TPU v7x, 256 devices: a whole 4x4x8 slice. The times are simulated.
256 devices in a mesh: spec: 8 (over x, core), space: 32 (over y, z).
Axes of the slice: x: 4, y: 4, z: 8, core: 2. Of those that a mesh axis runs over, the one named last changes fastest.
Arguments:
- spectra: float32 [768, 256, 128], P(None, ('space', 'spec')), may hold values from -6 to 6
- quad_first: bfloat16 [768, 768], replicated, may hold values from -0.21875 to 0.21875
- quad_second: bfloat16 [768, 768], replicated, may hold values from -0.21875 to 0.21875
- quad_output: bfloat16 [768, 768], replicated, may hold values from -0.21875 to 0.21875
- owner_map: int32 [32], replicated, may hold values from 0 to 2
- land_mask: int32 [256, 128], P('space'), may hold values 0 or 1
- nest_dest: int32 [8192], P('space'), may hold values from 0 to 31, as said below
- nest_src: int32 [8192], P('space'), may hold values from 0 to 1023
- nest_into: int32 [8192], P('space'), may hold values from 0 to 1023
Outputs:
- spectra_out: float32 [768, 256, 128], P(None, ('space', 'spec'))
Inputs may be any that keep to these rules, and one draw needn't show every extreme that they name: `nest_dest`: among the 256 entries of each tile no tile is named more than 16 times, and one tile is named exactly 16 times by the entries of every tile.
All inputs are finite; a program needn't handle non-finite values. No bound on the sum of `land_mask` on one device may be relied on, other than what follows from the above.
Results may differ from a plain program's by a relative error of at most 0.0016.
Values sent between devices are 32-bit elements; how exact they have to be, the bound alone decides.
No kernel may reach another device: no remote copies, remote signals or barrier semaphores. Data moves between devices by JAX's collectives and lax.ppermute only.
A program may use at most 64 MiB of HBM per device.

v0:
```python
import math

import jax
import jax.numpy as jnp
from jax import lax
from jax.sharding import PartitionSpec as P

DIRS = 24
SUBSTEPS = 6
CAP = 16
FREQS = 32


step_weight = 0.25
grid_factors = (1.0, 0.55, 0.3)


def padded_2(value, sides, width):
    for axis, dim in sides:
        devices, length = (lax.axis_size(axis), value.shape[dim])
        up = [(i, (i + 1) % devices) for i in range(devices - 1)]
        down = [(j, i) for i, j in up]
        last = lax.slice_in_dim(value, length - width, length, axis=dim)
        leading = lax.slice_in_dim(value, 0, width, axis=dim)
        before = lax.ppermute(last, axis, up)
        after = lax.ppermute(leading, axis, down)
        value = jnp.concatenate([before, value, after], axis=dim)
    return value


def minmod(lower_diff, upper_diff):
    return (
        0.5
        * (jnp.sign(lower_diff) + jnp.sign(upper_diff))
        * jnp.minimum(jnp.abs(lower_diff), jnp.abs(upper_diff))
    )


def upwind_sweep(padded, courant, forward, axis_index):
    length = padded.shape[axis_index]
    differences = lax.slice_in_dim(padded, 1, length, axis=axis_index) - lax.slice_in_dim(
        padded, 0, length - 1, axis=axis_index
    )
    slopes = minmod(
        lax.slice_in_dim(differences, 0, length - 2, axis=axis_index),
        lax.slice_in_dim(differences, 1, length - 1, axis=axis_index),
    )
    centres = lax.slice_in_dim(padded, 1, length - 1, axis=axis_index)
    upper_flux = courant * (centres + 0.5 * (1.0 - courant) * slopes)
    lower_flux = courant * (centres - 0.5 * (1.0 + courant) * slopes)
    face_count = length - 3
    fluxes = jnp.where(
        forward,
        lax.slice_in_dim(upper_flux, 0, face_count, axis=axis_index),
        lax.slice_in_dim(lower_flux, 1, face_count + 1, axis=axis_index),
    )
    interior = lax.slice_in_dim(padded, 2, length - 2, axis=axis_index)
    return interior - (
        lax.slice_in_dim(fluxes, 1, face_count, axis=axis_index)
        - lax.slice_in_dim(fluxes, 0, face_count - 1, axis=axis_index)
    )


def bin_speeds(first_bin, bin_count):
    indices = first_bin + jnp.arange(bin_count, dtype=jnp.int32)
    freq_index = (indices // DIRS).astype(jnp.float32)
    direction = ((indices % DIRS).astype(jnp.float32) + 0.5) * (2.0 * math.pi / DIRS)
    speeds = 0.2 + 0.7 * (freq_index + 0.5) / FREQS
    return (speeds * jnp.cos(direction), speeds * jnp.sin(direction))


def row_scales(owner_map, first_row, row_count, tile_rows):
    rows_here = first_row + jnp.arange(row_count, dtype=jnp.int32)
    tile_of = jnp.clip(rows_here // tile_rows, 0, owner_map.shape[0] - 1)
    matches = tile_of[:, None] == jnp.arange(owner_map.shape[0], dtype=jnp.int32)[None, :]
    grid_of = jnp.sum(jnp.where(matches, owner_map[None, :], 0), axis=1)
    scales = jnp.where(
        grid_of == 0, grid_factors[0], jnp.where(grid_of == 1, grid_factors[1], grid_factors[2])
    )
    return scales.astype(jnp.float32)


def substep(padded, scales, sea_rows, north_speed, east_speed):
    lat_courant = north_speed[:, None, None] * scales[None, 1:-1, None]
    advected = upwind_sweep(padded, lat_courant, (north_speed > 0)[:, None, None], 1)
    lon_padded = jnp.concatenate([advected[:, :, -2:], advected, advected[:, :, :2]], axis=2)
    lon_courant = east_speed[:, None, None] * scales[None, 2:-2, None]
    advected = upwind_sweep(lon_padded, lon_courant, (east_speed > 0)[:, None, None], 2)
    return advected * sea_rows[None]


def source_update(state_field, quad_first, quad_second, quad_output):
    contract = (((0,), (0,)), ((), ()))
    outline = state_field.shape
    matrix = state_field.reshape(outline[0], -1)
    rounded = matrix.astype(jnp.bfloat16)
    linear_one = lax.dot_general(quad_first, rounded, contract, preferred_element_type=jnp.float32)
    linear_two = lax.dot_general(quad_second, rounded, contract, preferred_element_type=jnp.float32)
    product = (linear_one * linear_two).astype(jnp.bfloat16)
    tendency = lax.dot_general(quad_output, product, contract, preferred_element_type=jnp.float32)
    return (matrix + step_weight * tendency).reshape(outline)


def shards(
    spectra,
    quad_first,
    quad_second,
    quad_output,
    owner_map,
    land_mask,
    nest_dest,
    nest_src,
    nest_into,
):
    spec_count = lax.axis_size("spec")
    tile_count = lax.axis_size("space")
    spec_rank = lax.axis_index("spec")
    tile_rank = lax.axis_index("space")
    lon_cols = spectra.shape[2]
    band_bins = spectra.shape[0] // spec_count
    sea_tile = land_mask.astype(jnp.float32)
    own_row = lax.dynamic_slice_in_dim(sea_tile, spec_rank, 1, 0)
    sourced = source_update(spectra, quad_first, quad_second, quad_output) * own_row[None]
    banded = lax.all_to_all(sourced, "spec", split_axis=0, concat_axis=1, tiled=True)
    north_speed, east_speed = bin_speeds(spec_rank * band_bins, band_bins)
    top_row = tile_rank * spec_count
    scales = row_scales(owner_map, top_row - 2, spec_count + 4, spec_count)
    for counter in range(SUBSTEPS):
        padded = padded_2(banded, (("space", 1),), 2)
        banded = substep(padded, scales, sea_tile, north_speed, east_speed)
    points = spec_count * lon_cols
    flat_field = banded.reshape(band_bins, points)
    slot_total = tile_count * CAP
    onehot = (nest_dest[:, None] == jnp.arange(tile_count, dtype=jnp.int32)[None, :]).astype(
        jnp.int32
    )
    slot_rank = jnp.sum(jnp.cumsum(onehot, axis=0) * onehot, axis=1) - 1
    slot_place = nest_dest * CAP + slot_rank
    outgoing = (
        jnp.zeros((band_bins, slot_total), jnp.float32)
        .at[:, slot_place]
        .set(flat_field[:, nest_src])
    )
    targets = jnp.full((1, slot_total), -1, jnp.int32).at[0, slot_place].set(nest_into)
    received, landing = (
        lax.all_to_all(outgoing, "space", split_axis=1, concat_axis=1, tiled=True),
        lax.all_to_all(targets, "space", split_axis=1, concat_axis=1, tiled=True),
    )
    usable = landing[0] >= 0
    target_point = jnp.where(usable, landing[0], 0)
    weights = usable.astype(jnp.float32)
    totals = (
        jnp.zeros((band_bins, points), jnp.float32)
        .at[:, target_point]
        .add(received * weights[None, :])
    )
    counts = jnp.zeros((points,), jnp.float32).at[target_point].add(weights)
    merged = (flat_field + totals) / (1.0 + counts)[None, :]
    finished = source_update(
        lax.all_to_all(
            merged.reshape(band_bins, spec_count, lon_cols),
            "spec",
            split_axis=1,
            concat_axis=0,
            tiled=True,
        ),
        quad_first,
        quad_second,
        quad_output,
    )
    return finished * own_row[None]


def solution(mesh):
    return jax.shard_map(
        shards,
        mesh=mesh,
        in_specs=(
            P(None, ("space", "spec"), None),
            P(),
            P(),
            P(),
            P(),
            P("space", None),
            P("space"),
            P("space"),
            P("space"),
        ),
        out_specs=P(None, ("space", "spec"), None),
        check_vma=False,
    )
```

profile of v0, /device:TPU:1, one launch (start us, length us, event | category | flops | bytes accessed | tf_op | source)
XLA Modules:
  0.0 160.3 jit_solution(9757254583475292669)
XLA Ops:
  0.8 2.0 %copy.30 = f32[768,1,128]{0,2,1:T(8,128)} copy(f32[768,1,128]{2,1,0:T(1,128)} %param.9) | data formatting | bytes 786432 | tf_op args[0]
  2.8 2.3 %fusion.102 = f32[768,128]{1,0:T(8,128)} fusion(bf16[768,768]{1,0:T(8,128)(2,1)S(1)} %copy-done, f32[768,1,128]{0,2,1:T(8,128)} %copy.30), kind=kOutput, calls=%fused_computation.241 | convolution fusion | flops 150994944 | bytes 1966080 | tf_op jit(solution)/shard_map/dot_general | solution.py:97
  5.1 3.0 %fusion.4 = f32[768,1,128]{0,2,1:T(8,128)} fusion(bf16[768,768]{1,0:T(8,128)(2,1)S(1)} %copy-done.1, f32[768,128]{1,0:T(8,128)} %fusion.102, bf16[768,768]{1,0:T(8,128)(2,1)S(1)} %copy-done.2, f32[768,1,128]{0,2,1:T(8,128)} %copy.30, f32[128]{0:T(128)S(1)} %dynamic-slice_bitcast_fusion), kind=kOutput, calls=%fused_computation.13 | convolution fusion | flops 302481408 | bytes 3539456 | tf_op jit(solution)/shard_map/dot_general | solution.py:100
  10.1 6.6 %all-to-all-start = ((f32[768,1,128]{2,1,0:T(1,128)}), f32[768,1,128]{2,1,0:T(1,128)S(1)}, u32[]{:S(2)}, u32[]{:S(2)}) async-start(f32[768,1,128]{2,1,0:T(1,128)} %copy.31), calls=%async_computation | async-start | bytes 786432 | tf_op jit(solution)/shard_map/all_to_all | solution.py:124
  17.9 6.5 %all-to-all-done = f32[768,1,128]{2,1,0:T(1,128)S(1)} async-done(((f32[768,1,128]{2,1,0:T(1,128)}), f32[768,1,128]{2,1,0:T(1,128)S(1)}, u32[]{:S(2)}, u32[]{:S(2)}) %all-to-all-start) | async-done | bytes 393248 | tf_op jit(solution)/shard_map/all_to_all | solution.py:124
  24.4 2.8 %collective-permute-start = (f32[96,2,128]{2,0,1:T(8,128)S(1)}, f32[96,2,128]{2,0,1:T(8,128)S(1)}, u32[]{:S(2)}, u32[]{:S(2)}) collective-permute-start(f32[96,2,128]{2,0,1:T(8,128)S(1)} %get-tuple-element.27), channel_id=1, source_target_pairs={{0,1},{1,2},{2,3},{3,4},{4,5},{5,6},{6,7},{7,8},{8,9},{9,10},{10,1... | collective-permute-start | bytes 294920 | tf_op jit(solution)/shard_map/ppermute | solution.py:25
  28.8 3.9 %collective-permute-done.1 = f32[96,2,128]{2,0,1:T(8,128)S(1)} collective-permute-done((f32[96,2,128]{2,0,1:T(8,128)S(1)}, f32[96,2,128]{2,0,1:T(8,128)S(1)}, u32[]{:S(2)}, u32[]{:S(2)}) %collective-permute-start.1) | collective-permute-done | bytes 98336 | tf_op jit(solution)/shard_map/ppermute | solution.py:26
  36.3 3.5 %collective-permute-start.2 = (f32[96,2,128]{2,0,1:T(8,128)S(1)}, f32[96,2,128]{2,0,1:T(8,128)S(1)}, u32[]{:S(2)}, u32[]{:S(2)}) collective-permute-start(f32[96,2,128]{2,0,1:T(8,128)S(1)} %get-tuple-element.23), channel_id=1, source_target_pairs={{0,1},{1,2},{2,3},{3,4},{4,5},{5,6},{6,7},{7,8},{8,9},{9,10},{10,1... | collective-permute-start | bytes 294920 | tf_op jit(solution)/shard_map/ppermute | solution.py:25
  41.5 5.1 %collective-permute-done.3 = f32[96,2,128]{2,0,1:T(8,128)S(1)} collective-permute-done((f32[96,2,128]{2,0,1:T(8,128)S(1)}, f32[96,2,128]{2,0,1:T(8,128)S(1)}, u32[]{:S(2)}, u32[]{:S(2)}) %collective-permute-start.3) | collective-permute-done | bytes 98336 | tf_op jit(solution)/shard_map/ppermute | solution.py:26
  50.3 4.6 %collective-permute-start.4 = (f32[96,2,128]{2,0,1:T(8,128)S(1)}, f32[96,2,128]{2,0,1:T(8,128)S(1)}, u32[]{:S(2)}, u32[]{:S(2)}) collective-permute-start(f32[96,2,128]{2,0,1:T(8,128)S(1)} %get-tuple-element.19), channel_id=1, source_target_pairs={{0,1},{1,2},{2,3},{3,4},{4,5},{5,6},{6,7},{7,8},{8,9},{9,10},{10,1... | collective-permute-start | bytes 294920 | tf_op jit(solution)/shard_map/ppermute | solution.py:25
  56.5 3.7 %collective-permute-done.5 = f32[96,2,128]{2,0,1:T(8,128)S(1)} collective-permute-done((f32[96,2,128]{2,0,1:T(8,128)S(1)}, f32[96,2,128]{2,0,1:T(8,128)S(1)}, u32[]{:S(2)}, u32[]{:S(2)}) %collective-permute-start.5) | collective-permute-done | bytes 98336 | tf_op jit(solution)/shard_map/ppermute | solution.py:26
  63.9 3.7 %collective-permute-start.6 = (f32[96,2,128]{2,0,1:T(8,128)S(1)}, f32[96,2,128]{2,0,1:T(8,128)S(1)}, u32[]{:S(2)}, u32[]{:S(2)}) collective-permute-start(f32[96,2,128]{2,0,1:T(8,128)S(1)} %get-tuple-element.15), channel_id=1, source_target_pairs={{0,1},{1,2},{2,3},{3,4},{4,5},{5,6},{6,7},{7,8},{8,9},{9,10},{10,1... | collective-permute-start | bytes 294920 | tf_op jit(solution)/shard_map/ppermute | solution.py:25
  71.1 9.0 %all-to-all-start.1 = ((s32[1,32,16]{2,0,1:T(1,128)}), s32[1,32,16]{2,0,1:T(1,128)S(1)}, u32[]{:S(2)}, u32[]{:S(2)}) async-start(s32[1,32,16]{2,0,1:T(1,128)} %bitcast.12), calls=%async_computation.1 | async-start | bytes 32768 | tf_op jit(solution)/shard_map/all_to_all | solution.py:147
  83.8 3.1 %collective-permute-start.8 = (f32[96,2,128]{2,0,1:T(8,128)S(1)}, f32[96,2,128]{2,0,1:T(8,128)S(1)}, u32[]{:S(2)}, u32[]{:S(2)}) collective-permute-start(f32[96,2,128]{2,0,1:T(8,128)S(1)} %get-tuple-element.11), channel_id=1, source_target_pairs={{0,1},{1,2},{2,3},{3,4},{4,5},{5,6},{6,7},{7,8},{8,9},{9,10},{10,1... | collective-permute-start | bytes 294920 | tf_op jit(solution)/shard_map/ppermute | solution.py:25
  88.6 4.0 %collective-permute-done.9 = f32[96,2,128]{2,0,1:T(8,128)S(1)} collective-permute-done((f32[96,2,128]{2,0,1:T(8,128)S(1)}, f32[96,2,128]{2,0,1:T(8,128)S(1)}, u32[]{:S(2)}, u32[]{:S(2)}) %collective-permute-start.9) | collective-permute-done | bytes 98336 | tf_op jit(solution)/shard_map/ppermute | solution.py:26
  96.2 3.1 %collective-permute-start.10 = (f32[96,2,128]{2,0,1:T(8,128)S(1)}, f32[96,2,128]{2,0,1:T(8,128)S(1)}, u32[]{:S(2)}, u32[]{:S(2)}) collective-permute-start(f32[96,2,128]{2,0,1:T(8,128)S(1)} %get-tuple-element.7), channel_id=1, source_target_pairs={{0,1},{1,2},{2,3},{3,4},{4,5},{5,6},{6,7},{7,8},{8,9},{9,10},{10,1... | collective-permute-start | bytes 294920 | tf_op jit(solution)/shard_map/ppermute | solution.py:25
  101.0 4.1 %collective-permute-done.11 = f32[96,2,128]{2,0,1:T(8,128)S(1)} collective-permute-done((f32[96,2,128]{2,0,1:T(8,128)S(1)}, f32[96,2,128]{2,0,1:T(8,128)S(1)}, u32[]{:S(2)}, u32[]{:S(2)}) %collective-permute-start.11) | collective-permute-done | bytes 98336 | tf_op jit(solution)/shard_map/ppermute | solution.py:26
  108.9 2.6 %scatter_custom_fusion.1 = f32[96,512]{0,1:T(8,128)} fusion(s32[256]{0:T(256)S(1)} %compare_select_fusion.3, f32[96,1024]{0,1:T(8,128)S(1)} %bitcast.87, s32[1024]{0:T(1024)S(1)} %pad_clamp_fusion, f32[]{:T(128)} %constant.46.clone.1), kind=kCustom, calls=%fused_computation.175 | custom fusion | bytes 196612 | tf_op jit(solution)/shard_map/scatter | solution.py:142
  111.5 8.8 %all-to-all-start.2 = ((f32[96,32,16]{0,2,1:T(8,128)}), f32[96,32,16]{0,2,1:T(8,128)S(1)}, u32[]{:S(2)}, u32[]{:S(2)}) async-start(f32[96,32,16]{0,2,1:T(8,128)} %bitcast.14), calls=%async_computation.2 | async-start | bytes 524288 | tf_op jit(solution)/shard_map/all_to_all | solution.py:146
  121.8 4.1 %scatter_custom_fusion.3 = f32[1024]{0:T(1024)S(1)} fusion(s32[512]{0:T(512)S(1)} %bitcast.97, f32[512]{0:T(512)S(1)} %reshape.351, f32[]{:T(128)} %constant.98.clone.1), kind=kCustom, calls=%fused_computation.203 | custom fusion | flops 512 | bytes 4100 | tf_op jit(solution)/shard_map/scatter-add | solution.py:157
  125.9 4.1 %all-to-all-done.2 = f32[96,32,16]{0,2,1:T(8,128)S(1)} async-done(((f32[96,32,16]{0,2,1:T(8,128)}), f32[96,32,16]{0,2,1:T(8,128)S(1)}, u32[]{:S(2)}, u32[]{:S(2)}) %all-to-all-start.2) | async-done | bytes 196640 | tf_op jit(solution)/shard_map/all_to_all | solution.py:146
  130.1 3.5 %scatter_custom_fusion.2 = f32[96,1024]{0,1:T(8,128)S(1)} fusion(f32[96,1024]{0,1:T(8,128)S(1)} %bitcast.88, s32[512]{0:T(512)S(1)} %bitcast.98, f32[96,512]{0,1:T(8,128)S(1)} %bitcast_multiply_fusion), kind=kCustom, calls=%fused_computation.171 | custom fusion | flops 49152 | bytes 655360 | tf_op jit(solution)/shard_map/scatter-add | solution.py:155
  134.8 21.2 %all_to_all.54 = f32[96,8,128]{2,0,1:T(8,128)S(1)} all-to-all(f32[96,8,128]{2,0,1:T(8,128)} %copy.35), channel_id=1, replica_groups=mesh['spec'=8,'space'=32] {'spec'}, dimensions={1} | all-to-all | bytes 786432 | tf_op jit(solution)/shard_map/all_to_all | solution.py:160
  157.3 2.0 %fusion.7 = f32[768,1,128]{0,2,1:T(8,128)S(1)} fusion(f32[768,128]{0,1:T(8,128)S(1)} %copy.36, bf16[768,768]{1,0:T(8,128)(2,1)S(1)} %copy-done.1, f32[128,768]{1,0:T(8,128)} %fusion.72, bf16[768,768]{1,0:T(8,128)(2,1)} %param.11, f32[128]{0:T(128)S(1)} %dynamic-slice_bitcast_fusion, f32[768,128]{1,0:T(8,128)S(1)} %bitcast.83), kind=kOutput, calls=%fused_computation.16 | convolution fusion | flops 302579712 | bytes 3932672 | tf_op jit(solution)/shard_map/dot_general | solution.py:100
  (152 shorter events, 42.0 us)
Async XLA Ops:
  0.0 2.8 %copy-start = (bf16[768,768]{1,0:T(8,128)(2,1)S(1)}, bf16[768,768]{1,0:T(8,128)(2,1)}, u32[]{:S(2)}) copy-start(bf16[768,768]{1,0:T(8,128)(2,1)} %param.10) | copy-start | bytes 3538948
  0.8 4.3 %copy-start.2 = (bf16[768,768]{1,0:T(8,128)(2,1)S(1)}, bf16[768,768]{1,0:T(8,128)(2,1)}, u32[]{:S(2)}) copy-start(bf16[768,768]{1,0:T(8,128)(2,1)} %param.11) | copy-start | bytes 3538948
  2.8 2.4 %copy-start.1 = (bf16[768,768]{1,0:T(8,128)(2,1)S(1)}, bf16[768,768]{1,0:T(8,128)(2,1)}, u32[]{:S(2)}) copy-start(bf16[768,768]{1,0:T(8,128)(2,1)} %param.12) | copy-start | bytes 3538948
  8.2 8.5 %copy-start.6 = (s32[32]{0:T(128)S(1)}, s32[32]{0:T(128)}, u32[]{:S(2)}) copy-start(s32[32]{0:T(128)} %param.13) | copy-start | bytes 388
  8.2 8.9 %copy-start.3 = (s32[256]{0:T(256)S(1)}, s32[256]{0:T(256)}, u32[]{:S(2)}) copy-start(s32[256]{0:T(256)} %param.15) | copy-start | bytes 3076
  10.1 14.3 %all-to-all-start = ((f32[768,1,128]{2,1,0:T(1,128)}), f32[768,1,128]{2,1,0:T(1,128)S(1)}, u32[]{:S(2)}, u32[]{:S(2)}) async-start(f32[768,1,128]{2,1,0:T(1,128)} %copy.31), calls=%async_computation | async-start | bytes 786432 | tf_op jit(solution)/shard_map/all_to_all | solution.py:124
  24.4 4.4 %collective-permute-start = (f32[96,2,128]{2,0,1:T(8,128)S(1)}, f32[96,2,128]{2,0,1:T(8,128)S(1)}, u32[]{:S(2)}, u32[]{:S(2)}) collective-permute-start(f32[96,2,128]{2,0,1:T(8,128)S(1)} %get-tuple-element.27), channel_id=1, source_target_pairs={{0,1},{1,2},{2,3},{3,4},{4,5},{5,6},{6,7},{7,8},{8,9},{9,10},{10,1... | collective-permute-start | bytes 294920 | tf_op jit(solution)/shard_map/ppermute | solution.py:25
  27.1 5.5 %collective-permute-start.1 = (f32[96,2,128]{2,0,1:T(8,128)S(1)}, f32[96,2,128]{2,0,1:T(8,128)S(1)}, u32[]{:S(2)}, u32[]{:S(2)}) collective-permute-start(f32[96,2,128]{2,0,1:T(8,128)S(1)} %get-tuple-element.28), channel_id=1, source_target_pairs={{1,0},{2,1},{3,2},{4,3},{5,4},{6,5},{7,6},{8,7},{9,8},{10,9},{11,1... | collective-permute-start | bytes 294920 | tf_op jit(solution)/shard_map/ppermute | solution.py:26
  36.3 5.2 %collective-permute-start.2 = (f32[96,2,128]{2,0,1:T(8,128)S(1)}, f32[96,2,128]{2,0,1:T(8,128)S(1)}, u32[]{:S(2)}, u32[]{:S(2)}) collective-permute-start(f32[96,2,128]{2,0,1:T(8,128)S(1)} %get-tuple-element.23), channel_id=1, source_target_pairs={{0,1},{1,2},{2,3},{3,4},{4,5},{5,6},{6,7},{7,8},{8,9},{9,10},{10,1... | collective-permute-start | bytes 294920 | tf_op jit(solution)/shard_map/ppermute | solution.py:25
  39.9 6.8 %collective-permute-start.3 = (f32[96,2,128]{2,0,1:T(8,128)S(1)}, f32[96,2,128]{2,0,1:T(8,128)S(1)}, u32[]{:S(2)}, u32[]{:S(2)}) collective-permute-start(f32[96,2,128]{2,0,1:T(8,128)S(1)} %get-tuple-element.24), channel_id=1, source_target_pairs={{1,0},{2,1},{3,2},{4,3},{5,4},{6,5},{7,6},{8,7},{9,8},{10,9},{11,1... | collective-permute-start | bytes 294920 | tf_op jit(solution)/shard_map/ppermute | solution.py:26
  41.4 5.3 %copy-start.4 = (s32[32,3]{0,1:T(4,128)}, s32[32,3]{0,1:T(4,128)S(1)}, u32[]{:S(2)}) copy-start(s32[32,3]{0,1:T(4,128)S(1)} %reduce-window.9) | copy-start | bytes 1156
  50.1 6.3 %slice-start = ((s32[32,3]{0,1:T(4,128)}), s32[32,2]{0,1:T(2,128)S(1)}, s32[]{:S(2)}) async-start(s32[32,3]{0,1:T(4,128)} %copy-done.4), calls=%async_computation.4 | async-start | bytes 2048 | tf_op jit(solution)/shard_map/slice.1
  50.3 6.2 %collective-permute-start.4 = (f32[96,2,128]{2,0,1:T(8,128)S(1)}, f32[96,2,128]{2,0,1:T(8,128)S(1)}, u32[]{:S(2)}, u32[]{:S(2)}) collective-permute-start(f32[96,2,128]{2,0,1:T(8,128)S(1)} %get-tuple-element.19), channel_id=1, source_target_pairs={{0,1},{1,2},{2,3},{3,4},{4,5},{5,6},{6,7},{7,8},{8,9},{9,10},{10,1... | collective-permute-start | bytes 294920 | tf_op jit(solution)/shard_map/ppermute | solution.py:25
  54.9 5.4 %collective-permute-start.5 = (f32[96,2,128]{2,0,1:T(8,128)S(1)}, f32[96,2,128]{2,0,1:T(8,128)S(1)}, u32[]{:S(2)}, u32[]{:S(2)}) collective-permute-start(f32[96,2,128]{2,0,1:T(8,128)S(1)} %get-tuple-element.20), channel_id=1, source_target_pairs={{1,0},{2,1},{3,2},{4,3},{5,4},{6,5},{7,6},{8,7},{9,8},{10,9},{11,1... | collective-permute-start | bytes 294920 | tf_op jit(solution)/shard_map/ppermute | solution.py:26
  63.9 16.3 %collective-permute-start.6 = (f32[96,2,128]{2,0,1:T(8,128)S(1)}, f32[96,2,128]{2,0,1:T(8,128)S(1)}, u32[]{:S(2)}, u32[]{:S(2)}) collective-permute-start(f32[96,2,128]{2,0,1:T(8,128)S(1)} %get-tuple-element.15), channel_id=1, source_target_pairs={{0,1},{1,2},{2,3},{3,4},{4,5},{5,6},{6,7},{7,8},{8,9},{9,10},{10,1... | collective-permute-start | bytes 294920 | tf_op jit(solution)/shard_map/ppermute | solution.py:25
  67.5 12.6 %collective-permute-start.7 = (f32[96,2,128]{2,0,1:T(8,128)S(1)}, f32[96,2,128]{2,0,1:T(8,128)S(1)}, u32[]{:S(2)}, u32[]{:S(2)}) collective-permute-start(f32[96,2,128]{2,0,1:T(8,128)S(1)} %get-tuple-element.16), channel_id=1, source_target_pairs={{1,0},{2,1},{3,2},{4,3},{5,4},{6,5},{7,6},{8,7},{9,8},{10,9},{11,1... | collective-permute-start | bytes 294920 | tf_op jit(solution)/shard_map/ppermute | solution.py:26
  71.1 40.4 %all-to-all-start.1 = ((s32[1,32,16]{2,0,1:T(1,128)}), s32[1,32,16]{2,0,1:T(1,128)S(1)}, u32[]{:S(2)}, u32[]{:S(2)}) async-start(s32[1,32,16]{2,0,1:T(1,128)} %bitcast.12), calls=%async_computation.1 | async-start | bytes 32768 | tf_op jit(solution)/shard_map/all_to_all | solution.py:147
  83.6 4.7 %copy-start.5 = (s32[256]{0:T(256)S(1)}, s32[256]{0:T(256)}, u32[]{:S(2)}) copy-start(s32[256]{0:T(256)} %param.16) | copy-start | bytes 3076
  83.8 4.8 %collective-permute-start.8 = (f32[96,2,128]{2,0,1:T(8,128)S(1)}, f32[96,2,128]{2,0,1:T(8,128)S(1)}, u32[]{:S(2)}, u32[]{:S(2)}) collective-permute-start(f32[96,2,128]{2,0,1:T(8,128)S(1)} %get-tuple-element.11), channel_id=1, source_target_pairs={{0,1},{1,2},{2,3},{3,4},{4,5},{5,6},{6,7},{7,8},{8,9},{9,10},{10,1... | collective-permute-start | bytes 294920 | tf_op jit(solution)/shard_map/ppermute | solution.py:25
  87.0 5.7 %collective-permute-start.9 = (f32[96,2,128]{2,0,1:T(8,128)S(1)}, f32[96,2,128]{2,0,1:T(8,128)S(1)}, u32[]{:S(2)}, u32[]{:S(2)}) collective-permute-start(f32[96,2,128]{2,0,1:T(8,128)S(1)} %get-tuple-element.12), channel_id=1, source_target_pairs={{1,0},{2,1},{3,2},{4,3},{5,4},{6,5},{7,6},{8,7},{9,8},{10,9},{11,1... | collective-permute-start | bytes 294920 | tf_op jit(solution)/shard_map/ppermute | solution.py:26
  96.2 4.8 %collective-permute-start.10 = (f32[96,2,128]{2,0,1:T(8,128)S(1)}, f32[96,2,128]{2,0,1:T(8,128)S(1)}, u32[]{:S(2)}, u32[]{:S(2)}) collective-permute-start(f32[96,2,128]{2,0,1:T(8,128)S(1)} %get-tuple-element.7), channel_id=1, source_target_pairs={{0,1},{1,2},{2,3},{3,4},{4,5},{5,6},{6,7},{7,8},{8,9},{9,10},{10,1... | collective-permute-start | bytes 294920 | tf_op jit(solution)/shard_map/ppermute | solution.py:25
  99.4 5.7 %collective-permute-start.11 = (f32[96,2,128]{2,0,1:T(8,128)S(1)}, f32[96,2,128]{2,0,1:T(8,128)S(1)}, u32[]{:S(2)}, u32[]{:S(2)}) collective-permute-start(f32[96,2,128]{2,0,1:T(8,128)S(1)} %get-tuple-element.8), channel_id=1, source_target_pairs={{1,0},{2,1},{3,2},{4,3},{5,4},{6,5},{7,6},{8,7},{9,8},{10,9},{11,1... | collective-permute-start | bytes 294920 | tf_op jit(solution)/shard_map/ppermute | solution.py:26
  111.5 18.5 %all-to-all-start.2 = ((f32[96,32,16]{0,2,1:T(8,128)}), f32[96,32,16]{0,2,1:T(8,128)S(1)}, u32[]{:S(2)}, u32[]{:S(2)}) async-start(f32[96,32,16]{0,2,1:T(8,128)} %bitcast.14), calls=%async_computation.2 | async-start | bytes 524288 | tf_op jit(solution)/shard_map/all_to_all | solution.py:146
where the time goes:
time: 161 us; the launch traced here: 160 us
  starting transfers between devices  53.4 us (33%)
  waiting for transfers between devices  32.3 us (20%)
  other arithmetic  29 us (18%)
  blocking collectives  21.2 us (13%)
  local copies, waits for them, and re-layouts  15.1 us (9%)
  matrix products  8.51 us (5%)
    all_to_all x1, blocking collectives, shards(): lax.all_to_all(merged.reshape(band_bins, spec_count, lon_cols), 'spec', s...  21.2 us
    ppermute x6, waiting for transfers between devices, padded_2(): after = lax.ppermute(leading, axis, down)  21 us
    ppermute x6, starting transfers between devices, padded_2(): before = lax.ppermute(last, axis, up)  20.8 us
    all_to_all x1, starting transfers between devices, shards(): lax.all_to_all(targets, 'space', split_axis=1, concat_axis=1, tiled=True)  9.05 us
    all_to_all x1, starting transfers between devices, shards(): lax.all_to_all(outgoing, 'space', split_axis=1, concat_axis=1, tiled=True)  8.81 us
    ppermute x6, starting transfers between devices, padded_2(): after = lax.ppermute(leading, axis, down)  8.15 us
    select_n x12, other arithmetic, upwind_sweep(): jnp.where(forward, lax.slice_in_dim(upper_flux, 0, face_count, axis=axis_...  8.07 us
    all_to_all x1, starting transfers between devices, shards(): lax.all_to_all(sourced, 'spec', split_axis=0, concat_axis=1, tiled=True)  6.56 us
  transfers between devices with their start and end apart: 15, of which 11 were waited for; matrix products, arithmetic and copies ran while one was open for 14% of the time, Pallas kernels for 0%

commit v1 on v0

v1 whole, which is shorter than its diff:
```python
import math

import jax
import jax.numpy as jnp
from jax import lax
from jax.experimental import pallas as pl
from jax.experimental.pallas import tpu as pltpu
from jax.sharding import PartitionSpec as P

DIRS = 24
SUBSTEPS = 6
FREQS = 32
BINS = 768
LON = 128
LAT = 256
TILES = 32
ROWS = 8
OWN = 3
AUX = 12
STEPS = 32
step_weight = 0.25
grid_factors = (1.0, 0.55, 0.3)


def source_kernel(rank, field, mask, first_hbm, second_hbm, output_hbm, out, first, second, output, sems):
    copies = [
        pltpu.make_async_copy(src, dst, sems.at[n])
        for n, (src, dst) in enumerate(((first_hbm, first), (second_hbm, second), (output_hbm, output)))
    ]
    for copy in copies:
        copy.start()
    state = field[...]
    rounded = state.T.astype(jnp.bfloat16)
    copies[0].wait()
    one = jnp.dot(rounded, first[...], preferred_element_type=jnp.float32)
    copies[1].wait()
    two = jnp.dot(rounded, second[...], preferred_element_type=jnp.float32)
    product = (one * two).astype(jnp.bfloat16)
    copies[2].wait()
    tendency = jnp.dot(product, output[...], preferred_element_type=jnp.float32)
    sea = mask[pl.ds(rank[0], 1), :].astype(jnp.float32)
    out[...] = (state + step_weight * tendency.T) * sea


def source_update(rank, field, mask, quad_first, quad_second, quad_output):
    hbm = pl.BlockSpec(memory_space=pl.ANY)
    vmem = pl.BlockSpec(memory_space=pltpu.VMEM)
    return pl.pallas_call(
        source_kernel,
        out_shape=jax.ShapeDtypeStruct((BINS, LON), jnp.float32),
        in_specs=[pl.BlockSpec(memory_space=pltpu.SMEM), vmem, vmem, hbm, hbm, hbm],
        out_specs=vmem,
        scratch_shapes=[pltpu.VMEM((BINS, BINS), jnp.bfloat16)] * 3 + [pltpu.SemaphoreType.DMA((3,))],
        compiler_params=pltpu.CompilerParams(vmem_limit_bytes=16 * 2**20),
    )(rank, field, mask, quad_first, quad_second, quad_output)


def minmod(lower, upper):
    return jnp.maximum(jnp.minimum(upper, jnp.maximum(lower, 0.0)), jnp.minimum(lower, 0.0))


def transport_kernel(flags, field, aux, coefs, out, state, sea, weighted, columns, summed):
    north_forward = flags[0] > 0
    east_forward = flags[1] > 0
    upwind = jnp.where(east_forward, 1, LON - 1)
    downwind = LON - upwind

    def place(i):
        return jnp.where(north_forward, i, STEPS - 1 - i)

    sublane = lax.broadcasted_iota(jnp.int32, (8, LON), 0)

    def below(value):
        return jnp.where(sublane > 0, pltpu.roll(value, 1, 0), 0.0)

    def above(value):
        return jnp.where(sublane < 7, pltpu.roll(value, 7, 0), 0.0)

    def before(value):
        return jnp.where(north_forward, below(value), above(value))

    def after(value):
        return jnp.where(north_forward, above(value), below(value))

    for i in range(STEPS):
        sea[place(i)] = aux[pl.ds(AUX * (i // 8) + i % 8, 8, stride=AUX * 4), :].astype(jnp.float32)
        for q in range(OWN):
            state[place(i), q] = field[pl.ds(OWN * i + q, 8, stride=OWN * STEPS), :]

    def coef(kind, q, i):
        return coefs[pl.ds(((kind * OWN + q) * 4 + i // 8) * 8, 8), :]

    def flux(kind, q, i, value, slope):
        return coef(kind, q, i) * value + coef(kind + 1, q, i) * slope

    def substep(step, carry):
        here, prev, last, flow = [], [], [], []
        for q in range(OWN):
            start = state[0, q]
            end = state[STEPS - 1, q]
            beyond = after(start)
            slope = minmod(end - state[STEPS - 2, q], beyond - end)
            here.append(start)
            prev.append(start - before(end))
            last.append(beyond)
            flow.append(before(flux(0, q, STEPS - 1, end, slope)))
        for i in range(STEPS):
            for q in range(OWN):
                upper = state[i + 1, q] if i + 1 < STEPS else last[q]
                diff = upper - here[q]
                leaving = flux(0, q, i, here[q], minmod(prev[q], diff))
                value = here[q] - leaving + flow[q]
                here[q], prev[q], flow[q] = upper, diff, leaving
                lower = value - pltpu.roll(value, upwind, 1)
                higher = pltpu.roll(value, downwind, 1) - value
                leaving = flux(2, q, i, value, minmod(lower, higher))
                value = value - leaving + pltpu.roll(leaving, upwind, 1)
                state[i, q] = value * sea[i]
        return carry

    lax.fori_loop(0, SUBSTEPS, substep, 0)

    low_index = lax.broadcasted_iota(jnp.int32, (128, LON), 0)
    high_index = lax.broadcasted_iota(jnp.int32, (256, LON), 0)
    for j in range(4):
        for half in range(2):
            source = aux[pl.ds(AUX * j + 8 + half, 8, stride=AUX * 4), :]
            target = aux[pl.ds(AUX * j + 10 + half, 8, stride=AUX * 4), :]
            source_row = source // LON
            source_col = source % LON
            target_row = target // LON
            target_step = target_row % STEPS
            low = (target_step % 16) * 8 + target_row // STEPS
            high = (target_step // 16) * LON + target % LON
            pieces = []
            for q in range(OWN):
                taken = jnp.zeros((8, LON), jnp.float32)
                for r in range(ROWS):
                    row = state[place(8 * j + r), q]
                    taken = jnp.where(source_row == r, jnp.take_along_axis(row, source_col, axis=1), taken)
                coarse = taken.astype(jnp.bfloat16)
                wide = coarse.astype(jnp.float32)
                pieces += [wide, taken - wide]
            pieces.append(jnp.ones((8, LON), jnp.float32))
            for g in range(8):
                at = ((j * 2 + half) * 8 + g) * LON
                hit = low_index == low[g : g + 1, :]
                for n, piece in enumerate(pieces):
                    chosen = jnp.where(hit, piece[g : g + 1, :], 0.0)
                    weighted[n * 128 : n * 128 + 128, at : at + LON] = chosen.astype(jnp.bfloat16)
                hit = high_index == high[g : g + 1, :]
                columns[:, at : at + LON] = jnp.where(hit, 1.0, 0.0).astype(jnp.bfloat16)
    summed[...] = lax.dot_general(
        weighted[...], columns[...], (((1,), (1,)), ((), ())), preferred_element_type=jnp.float32
    )
    for i in range(STEPS):
        top = (i % 16) * 8
        left = (i // 16) * LON

        def block(n):
            return summed[n * 128 + top : n * 128 + top + 8, left : left + LON]

        share = 1.0 / (1.0 + block(2 * OWN))
        for q in range(OWN):
            merged = (state[place(i), q] + (block(2 * q) + block(2 * q + 1))) * share
            out[pl.ds(OWN * i + q, 8, stride=OWN * STEPS), :] = merged


def transport(flags, field, aux, coefs):
    vmem = pl.BlockSpec(memory_space=pltpu.VMEM)
    entries = TILES * LAT
    return pl.pallas_call(
        transport_kernel,
        out_shape=jax.ShapeDtypeStruct((BINS, LON), jnp.float32),
        in_specs=[pl.BlockSpec(memory_space=pltpu.SMEM), vmem, vmem, vmem],
        out_specs=vmem,
        scratch_shapes=[
            pltpu.VMEM((STEPS, OWN, 8, LON), jnp.float32),
            pltpu.VMEM((STEPS, 8, LON), jnp.float32),
            pltpu.VMEM(((2 * OWN + 1) * 128, entries), jnp.bfloat16),
            pltpu.VMEM((256, entries), jnp.bfloat16),
            pltpu.VMEM(((2 * OWN + 1) * 128, 256), jnp.float32),
        ],
        compiler_params=pltpu.CompilerParams(vmem_limit_bytes=40 * 2**20),
    )(flags, field, aux, coefs)


def bin_speeds(first_bin, bin_count):
    indices = first_bin + jnp.arange(bin_count, dtype=jnp.int32)
    freq_index = (indices // DIRS).astype(jnp.float32)
    direction = ((indices % DIRS).astype(jnp.float32) + 0.5) * (2.0 * math.pi / DIRS)
    speeds = 0.2 + 0.7 * (freq_index + 0.5) / FREQS
    return (speeds * jnp.cos(direction), speeds * jnp.sin(direction))


def shards(
    spectra,
    quad_first,
    quad_second,
    quad_output,
    owner_map,
    land_mask,
    nest_dest,
    nest_src,
    nest_into,
):
    everyone = ("space", "spec")
    spec_rank = lax.axis_index("spec")
    device = lax.axis_index("space") * lax.axis_size("spec") + spec_rank
    rank = spec_rank.reshape(1)
    target = nest_dest * (ROWS * LON) + nest_into
    lists = jnp.concatenate([land_mask.reshape(-1), nest_src, target])
    lists = jnp.broadcast_to(lists, (TILES, 1, AUX * LON))
    aux = lax.all_to_all(lists, "space", split_axis=0, concat_axis=0, tiled=True).reshape(TILES * AUX, LON)
    north, east = bin_speeds(device * OWN, OWN)
    flags = jnp.stack([north[0] > 0, east[0] > 0]).astype(jnp.int32)
    scales = jnp.where(
        owner_map == 0, grid_factors[0], jnp.where(owner_map == 1, grid_factors[1], grid_factors[2])
    ).astype(jnp.float32)
    scales = scales.reshape(8, 4).T
    scales = jnp.where(north[0] > 0, scales, scales[::-1])
    lat = jnp.abs(north)[:, None, None] * scales[None]
    lon = jnp.abs(east)[:, None, None] * scales[None]
    coefs = jnp.stack([lat, 0.5 * lat * (1.0 - lat), lon, 0.5 * lon * (1.0 - lon)])
    coefs = jnp.broadcast_to(coefs[..., None], coefs.shape + (LON,)).reshape(-1, LON)
    sourced = source_update(rank, spectra.reshape(BINS, LON), land_mask, quad_first, quad_second, quad_output)
    banded = lax.all_to_all(
        sourced.reshape(LAT, 1, OWN * LON), everyone, split_axis=0, concat_axis=0, tiled=True
    ).reshape(BINS, LON)
    merged = transport(flags, banded, aux, coefs)
    rows = lax.all_to_all(
        merged.reshape(LAT, 1, OWN * LON), everyone, split_axis=0, concat_axis=0, tiled=True
    ).reshape(BINS, LON)
    finished = source_update(rank, rows, land_mask, quad_first, quad_second, quad_output)
    return finished.reshape(BINS, 1, LON)


def solution(mesh):
    return jax.shard_map(
        shards,
        mesh=mesh,
        in_specs=(
            P(None, ("space", "spec"), None),
            P(),
            P(),
            P(),
            P(),
            P("space", None),
            P("space"),
            P("space"),
            P("space"),
        ),
        out_specs=P(None, ("space", "spec"), None),
        check_vma=False,
    )
```

time: 161 us -> 113 us (0.70)
  Pallas kernels: 0 us -> 34.8 us
  starting transfers between devices: 53.4 us -> 26.3 us
  other arithmetic: 29 us -> 3.54 us
  waiting for transfers between devices: 32.3 us -> 14.9 us
  matrix products: 8.51 us -> 0 us
  local copies, waits for them, and re-layouts: 15.1 us -> 9.02 us
  blocking collectives: 21.2 us -> 23.2 us
    pallas_call x0 -> x3, Pallas kernels: none -> 34.8 us  [the longest x1 29.2 us: transport(): pl.pallas_call(transport_kernel, out_shape=jax.ShapeDtypeStruct((BINS, LO...]
    ppermute x12 -> x0, starting transfers between devices: 29 us -> none  [the longest x6 20.8 us: padded_2(): before = lax.ppermute(last, axis, up)]
    ppermute x12 -> x0, waiting for transfers between devices: 21.7 us -> none  [the longest x6 21 us: padded_2(): after = lax.ppermute(leading, axis, down)]
    dot_general x4 -> x0, matrix products: 8.51 us -> none  [the longest x2 5.07 us: source_update(): lax.dot_general(quad_output, product, contract, preferred_element_type=jn...]
    scatter-add x2 -> x0, other arithmetic: 7.62 us -> none  [the longest x1 4.09 us: shards(): counts = jnp.zeros((points,), jnp.float32).at[target_point].add(weights)]
    select_n x16 -> x2, other arithmetic: 8.09 us -> 0.67 us  [the longest x1 0.66 us: shards(): jnp.where(owner_map == 0, grid_factors[0], jnp.where(owner_map == 1, grid...]
    mul x21 -> x1, other arithmetic: 5.88 us -> 0.08 us  [shards(): lat = jnp.abs(north)[:, None, None] * scales[None]]
    unnamed x15 -> x22, local copies, waits for them, and re-layouts: 2 us -> 7.08 us
  transfers between devices with their start and end apart: 15 -> 2, of which waited for: 11 -> 1; matrix products, arithmetic and copies ran while one was open for 14% -> 3% of each run, Pallas kernels for 0% -> 2%
where the time goes in v1:
time: 113 us
  Pallas kernels  34.8 us (31%)
  starting transfers between devices  26.3 us (23%)
  blocking collectives  23.2 us (21%)
  waiting for transfers between devices  14.9 us (13%)
  local copies, waits for them, and re-layouts  9.02 us (8%)
  other arithmetic  3.54 us (3%)
    pallas_call x1, Pallas kernels, transport(): pl.pallas_call(transport_kernel, out_shape=jax.ShapeDtypeStruct((BINS, LO...  29.2 us
    all_to_all x1, blocking collectives, shards(): lax.all_to_all(merged.reshape(LAT, 1, OWN * LON), everyone, split_axis=0,...  23.2 us
    all_to_all x1, waiting for transfers between devices, shards(): lax.all_to_all(sourced.reshape(LAT, 1, OWN * LON), everyone, split_axis=0...  14.9 us
    all_to_all x1, starting transfers between devices, shards(): lax.all_to_all(sourced.reshape(LAT, 1, OWN * LON), everyone, split_axis=0...  14.3 us
    all_to_all x1, starting transfers between devices, shards(): lax.all_to_all(lists, 'space', split_axis=0, concat_axis=0, tiled=True)  12 us
    unnamed x22, local copies, waits for them, and re-layouts  7.08 us
    pallas_call x2, Pallas kernels, source_update(): pl.pallas_call(source_kernel, out_shape=jax.ShapeDtypeStruct((BINS, LON),...  5.59 us
  transfers between devices with their start and end apart: 2, of which 1 were waited for; matrix products, arithmetic and copies ran while one was open for 3% of the time, Pallas kernels for 2%

profile of v1, /device:TPU:1, one launch (start us, length us, event | category | flops | bytes accessed | tf_op | source)
XLA Modules:
  0.0 112.6 jit_solution(2864357247469892640)
XLA Ops:
  0.0 0.7 multiply_add_fusion
  0.7 0.7 pad_add_fusion
  1.4 0.8 broadcast_in_dim.27
  2.2 12.0 %all-to-all-start.1 = ((s32[32,1,1536]{2,1,0:T(1,128)}), s32[32,1,1536]{2,1,0:T(1,128)S(1)}, u32[]{:S(2)}, u32[]{:S(2)}) async-start(s32[32,1,1536]{2,1,0:T(1,128)} %broadcast_in_dim.27), calls=%async_computation.1 | async-start | bytes 393216 | tf_op jit(solution)/shard_map/all_to_all | solution.py:214
  14.2 0.7 compare_select_fusion.1
  14.9 0.1 reshape.102
  15.0 0.6 sine_multiply_fusion
  15.7 1.3 %copy-done = bf16[768,768]{1,0:T(8,128)(2,1)S(1)} copy-done((bf16[768,768]{1,0:T(8,128)(2,1)S(1)}, bf16[768,768]{1,0:T(8,128)(2,1)}, u32[]{:S(2)}) %copy-start) | copy-done | bytes 1179672
  17.0 1.3 %copy-done.2 = bf16[768,768]{1,0:T(8,128)(2,1)S(1)} copy-done((bf16[768,768]{1,0:T(8,128)(2,1)S(1)}, bf16[768,768]{1,0:T(8,128)(2,1)}, u32[]{:S(2)}) %copy-start.2) | copy-done | bytes 1179672
  18.3 1.3 %copy-done.4 = bf16[768,768]{1,0:T(8,128)(2,1)S(1)} copy-done((bf16[768,768]{1,0:T(8,128)(2,1)S(1)}, bf16[768,768]{1,0:T(8,128)(2,1)}, u32[]{:S(2)}) %copy-start.4) | copy-done | bytes 1179672
  19.5 1.0 copy-done.8
  20.5 0.7 copy-done.9
  21.2 2.8 %shard_map.91 = f32[768,128]{1,0:T(8,128)} custom-call(s32[1]{0:T(128)} %bitcast.rank, f32[768,128]{1,0:T(8,128)S(1)} %bitcast.19, s32[8,128]{1,0:T(8,128)S(1)} %copy-done.9, bf16[768,768]{1,0:T(8,128)(2,1)S(1)} %copy-done, bf16[768,768]{1,0:T(8,128)(2,1)S(1)} %copy-done.2, bf16[768,768]{1,0:T(8,128)(2,1)S(1)} %copy-done.4), custom_call_target="tpu_custom_call" | custom-call | tf_op jit(solution)/shard_map/pallas_call | solution.py:48
  24.1 0.6 copy-done.6
  24.7 14.3 %all-to-all-start = ((f32[256,1,384]{2,1,0:T(1,128)}), f32[256,1,384]{2,1,0:T(1,128)}, u32[]{:S(2)}, u32[]{:S(2)}) async-start(f32[256,1,384]{2,1,0:T(1,128)} %bitcast.2), calls=%async_computation | async-start | bytes 786432 | tf_op jit(solution)/shard_map/all_to_all | solution.py:227
  39.0 0.1 copy.15
  39.2 0.6 pad_maximum_fusion
  39.8 0.8 broadcast_in_dim.31
  41.4 14.9 %all-to-all-done = f32[256,1,384]{2,1,0:T(1,128)} async-done(((f32[256,1,384]{2,1,0:T(1,128)}), f32[256,1,384]{2,1,0:T(1,128)}, u32[]{:S(2)}, u32[]{:S(2)}) %all-to-all-start) | async-done | bytes 393248 | tf_op jit(solution)/shard_map/all_to_all | solution.py:227
  56.3 0.1 broadcast_in_dim.32.coefs
  56.5 0.9 copy-done.7
  57.4 29.2 %shard_map.92 = f32[768,128]{1,0:T(8,128)S(1)} custom-call(s32[2]{0:T(128)S(1)} %add_convert_fusion.flags, f32[768,128]{1,0:T(8,128)} %bitcast.3.field, s32[384,128]{1,0:T(8,128)S(1)} %bitcast.18, f32[384,128]{1,0:T(8,128)S(1)} %broadcast_in_dim.32.coefs), custom_call_target="tpu_custom_call" | custom-call | tf_op jit(solution)/shard_map/pallas_call | solution.py:172
  86.6 23.2 %all_to_all.15 = f32[256,1,384]{2,1,0:T(1,128)S(1)} all-to-all(f32[256,1,384]{2,1,0:T(1,128)S(1)} %bitcast.16), channel_id=1, replica_groups=mesh['spec'=8,'space'=32] {'space','spec'}, dimensions={0} | all-to-all | bytes 786432 | tf_op jit(solution)/shard_map/all_to_all | solution.py:231
  109.8 2.8 %shard_map.93 = f32[768,128]{1,0:T(8,128)} custom-call(s32[1]{0:T(128)} %bitcast.rank, f32[768,128]{1,0:T(8,128)S(1)} %bitcast.17, s32[8,128]{1,0:T(8,128)S(1)} %copy-done.10, bf16[768,768]{1,0:T(8,128)(2,1)S(1)} %copy-done.1, bf16[768,768]{1,0:T(8,128)(2,1)S(1)} %copy-done.3, bf16[768,768]{1,0:T(8,128)(2,1)S(1)} %copy-done.5), custom_call_target="tpu_custom_call" | custom-call | tf_op jit(solution)/shard_map/pallas_call | solution.py:48
  (21 shorter events, 0.3 us)
Async XLA Ops:
  2.2 21.8 %all-to-all-start.1 = ((s32[32,1,1536]{2,1,0:T(1,128)}), s32[32,1,1536]{2,1,0:T(1,128)S(1)}, u32[]{:S(2)}, u32[]{:S(2)}) async-start(s32[32,1,1536]{2,1,0:T(1,128)} %broadcast_in_dim.27), calls=%async_computation.1 | async-start | bytes 393216 | tf_op jit(solution)/shard_map/all_to_all | solution.py:214
  15.7 1.3 %copy-start = (bf16[768,768]{1,0:T(8,128)(2,1)S(1)}, bf16[768,768]{1,0:T(8,128)(2,1)}, u32[]{:S(2)}) copy-start(bf16[768,768]{1,0:T(8,128)(2,1)} %first_hbm.3) | copy-start | bytes 3538948
  17.0 1.3 %copy-start.2 = (bf16[768,768]{1,0:T(8,128)(2,1)S(1)}, bf16[768,768]{1,0:T(8,128)(2,1)}, u32[]{:S(2)}) copy-start(bf16[768,768]{1,0:T(8,128)(2,1)} %second_hbm.3) | copy-start | bytes 3538948
  18.3 1.3 %copy-start.4 = (bf16[768,768]{1,0:T(8,128)(2,1)S(1)}, bf16[768,768]{1,0:T(8,128)(2,1)}, u32[]{:S(2)}) copy-start(bf16[768,768]{1,0:T(8,128)(2,1)} %output_hbm.3) | copy-start | bytes 3538948
  19.5 1.0 copy-start.8
  20.5 0.7 copy-start.9
  21.2 88.5 %copy-start.5 = (bf16[768,768]{1,0:T(8,128)(2,1)S(1)}, bf16[768,768]{1,0:T(8,128)(2,1)}, u32[]{:S(2)}) copy-start(bf16[768,768]{1,0:T(8,128)(2,1)} %output_hbm.3) | copy-start | bytes 3538948
  21.2 88.5 %copy-start.10 = (s32[8,128]{1,0:T(8,128)S(1)}, s32[8,128]{1,0:T(8,128)}, u32[]{:S(2)}) copy-start(s32[8,128]{1,0:T(8,128)} %mask.3) | copy-start | bytes 12292
  24.0 0.7 copy-start.6
  24.0 85.7 %copy-start.3 = (bf16[768,768]{1,0:T(8,128)(2,1)S(1)}, bf16[768,768]{1,0:T(8,128)(2,1)}, u32[]{:S(2)}) copy-start(bf16[768,768]{1,0:T(8,128)(2,1)} %second_hbm.3) | copy-start | bytes 3538948
  24.7 31.6 %all-to-all-start = ((f32[256,1,384]{2,1,0:T(1,128)}), f32[256,1,384]{2,1,0:T(1,128)}, u32[]{:S(2)}, u32[]{:S(2)}) async-start(f32[256,1,384]{2,1,0:T(1,128)} %bitcast.2), calls=%async_computation | async-start | bytes 786432 | tf_op jit(solution)/shard_map/all_to_all | solution.py:227
  39.0 70.8 %copy-start.1 = (bf16[768,768]{1,0:T(8,128)(2,1)S(1)}, bf16[768,768]{1,0:T(8,128)(2,1)}, u32[]{:S(2)}) copy-start(bf16[768,768]{1,0:T(8,128)(2,1)} %first_hbm.3) | copy-start | bytes 3538948
  56.5 0.9 copy-start.7

commit v2 on v1

v2 whole, which is shorter than its diff:
```python
import math

import jax
import jax.numpy as jnp
from jax import lax
from jax.experimental import pallas as pl
from jax.experimental.pallas import tpu as pltpu
from jax.sharding import PartitionSpec as P

DIRS = 24
SUBSTEPS = 6
FREQS = 32
BINS = 768
LON = 128
LAT = 256
ROWS = 8
ENTRIES = 8192
OWN = 3
SENT = 5
STEPS = 32
PIECES = 2 * OWN + 1
step_weight = 0.25
grid_factors = (1.0, 0.55, 0.3)


def tendency_of(state, first, second, output, wait):
    rounded = state.T.astype(jnp.bfloat16)
    wait(0)
    one = jnp.dot(rounded, first[...], preferred_element_type=jnp.float32)
    wait(1)
    two = jnp.dot(rounded, second[...], preferred_element_type=jnp.float32)
    product = (one * two).astype(jnp.bfloat16)
    wait(2)
    return jnp.dot(product, output[...], preferred_element_type=jnp.float32).T


def send_kernel(
    rank,
    field_hbm,
    mask_hbm,
    dest_hbm,
    src_hbm,
    into_hbm,
    first_hbm,
    second_hbm,
    output_hbm,
    out,
    field,
    mask,
    dest,
    src,
    into,
    first,
    second,
    output,
    sourced,
    sems,
):
    pairs = (
        (first_hbm, first),
        (second_hbm, second),
        (output_hbm, output),
        (field_hbm, field),
        (mask_hbm, mask),
        (dest_hbm, dest),
        (src_hbm, src),
        (into_hbm, into),
    )
    copies = [pltpu.make_async_copy(a, b, sems.at[n]) for n, (a, b) in enumerate(pairs)]
    for n in (3, 4, 5, 6, 7, 0, 1, 2):
        copies[n].start()
    for n in (3, 4, 5, 6, 7):
        copies[n].wait()
    state = field[...]
    sea = mask[pl.ds(rank[0], 1), :].astype(jnp.float32)
    part = rank[0] % 4
    wanted = lax.broadcasted_iota(jnp.int32, (2, LON), 0) == rank[0] // 4
    lane = lax.broadcasted_iota(jnp.int32, (8, LON), 1)

    def entries(value, shift):
        row = jnp.sum(jnp.where(wanted, value, 0), axis=0, keepdims=True).astype(jnp.float32)
        return pltpu.roll(jnp.broadcast_to(row, (8, LON)), shift, 1)

    lists = jnp.where(lane < 32, entries(src[...], (LON - 32 * part) % LON), 0.0)
    target = entries(dest[...] * (ROWS * LON) + into[...], (LON + 32 - 32 * part) % LON)
    lists = jnp.where((lane >= 32) & (lane < 64), target, lists)
    wide = jnp.broadcast_to(sea, (8, LON))
    for n in range(LAT // 8):
        out[pl.ds(SENT * 8 * n + OWN, 8, stride=SENT), :] = wide
        out[pl.ds(SENT * 8 * n + OWN + 1, 8, stride=SENT), :] = lists
    tendency = tendency_of(state, first, second, output, lambda n: copies[n].wait())
    sourced[...] = (state + step_weight * tendency) * sea
    for n in range(LAT // 8):
        for q in range(OWN):
            out[pl.ds(SENT * 8 * n + q, 8, stride=SENT), :] = sourced[pl.ds(OWN * 8 * n + q, 8, stride=OWN), :]


def source_and_pack(rank, field, mask, dest, src, into, first, second, output):
    hbm = pl.BlockSpec(memory_space=pltpu.HBM)
    square = pltpu.VMEM((BINS, BINS), jnp.bfloat16)
    pair = pltpu.VMEM((2, LON), jnp.int32)
    return pl.pallas_call(
        send_kernel,
        out_shape=jax.ShapeDtypeStruct((LAT * SENT, LON), jnp.float32),
        in_specs=[pl.BlockSpec(memory_space=pltpu.SMEM)] + [hbm] * 8,
        out_specs=pl.BlockSpec(memory_space=pltpu.VMEM),
        scratch_shapes=[
            pltpu.VMEM((BINS, LON), jnp.float32),
            pltpu.VMEM((ROWS, LON), jnp.int32),
            pair,
            pair,
            pair,
            square,
            square,
            square,
            pltpu.VMEM((BINS, LON), jnp.float32),
            pltpu.SemaphoreType.DMA((8,)),
        ],
        compiler_params=pltpu.CompilerParams(vmem_limit_bytes=62 * 2**20),
    )(rank, field, mask, dest, src, into, first, second, output)


def finish_kernel(rank, field, mask, first, second, output, out):
    state = field[...]
    sea = mask[pl.ds(rank[0], 1), :].astype(jnp.float32)
    out[...] = (state + step_weight * tendency_of(state, first, second, output, lambda n: None)) * sea


def source_update(rank, field, mask, first, second, output):
    vmem = pl.BlockSpec(memory_space=pltpu.VMEM)
    return pl.pallas_call(
        finish_kernel,
        out_shape=jax.ShapeDtypeStruct((BINS, LON), jnp.float32),
        in_specs=[pl.BlockSpec(memory_space=pltpu.SMEM)] + [vmem] * 5,
        out_specs=vmem,
        compiler_params=pltpu.CompilerParams(vmem_limit_bytes=16 * 2**20),
    )(rank, field, mask, first, second, output)


def minmod(lower, upper):
    return jnp.maximum(jnp.minimum(upper, jnp.maximum(lower, 0.0)), jnp.minimum(lower, 0.0))


def transport_kernel(device, owners, field, out, state, sea, coefs, weighted, columns, summed):
    first_bin = device[0] * OWN
    first_dir = first_bin % DIRS
    north_forward = (first_dir < DIRS // 4) | (first_dir >= DIRS - DIRS // 4)
    east_forward = first_dir < DIRS // 2
    upwind = jnp.where(east_forward, 1, LON - 1)
    downwind = LON - upwind

    def place(i):
        return jnp.where(north_forward, i, STEPS - 1 - i)

    def received(i, n):
        return field[pl.ds(SENT * i + n, 8, stride=SENT * STEPS), :]

    sublane = lax.broadcasted_iota(jnp.int32, (8, LON), 0)
    lane = lax.broadcasted_iota(jnp.int32, (8, LON), 1)

    def below(value):
        return jnp.where(sublane > 0, pltpu.roll(value, 1, 0), 0.0)

    def above(value):
        return jnp.where(sublane < 7, pltpu.roll(value, 7, 0), 0.0)

    def before(value):
        return jnp.where(north_forward, below(value), above(value))

    def after(value):
        return jnp.where(north_forward, above(value), below(value))

    for j in range(4):
        scale = jnp.zeros((8, LON), jnp.float32)
        for g in range(8):
            owner = owners[4 * g + jnp.where(north_forward, j, 3 - j)]
            factor = jnp.where(owner == 0, grid_factors[0], jnp.where(owner == 1, grid_factors[1], grid_factors[2]))
            scale = jnp.where(sublane == g, factor, scale)
        for q in range(OWN):
            splat = jnp.zeros((8, LON), jnp.int32) + (first_bin + q)
            direction = ((splat % DIRS).astype(jnp.float32) + 0.5) * (2.0 * math.pi / DIRS)
            speed = 0.2 + 0.7 * ((splat // DIRS).astype(jnp.float32) + 0.5) / FREQS
            north = jnp.abs(speed * jnp.cos(direction)) * scale
            east = jnp.abs(speed * jnp.sin(direction)) * scale
            for kind, value in enumerate(
                (north, 0.5 * north * (1.0 - north), east, 0.5 * east * (1.0 - east))
            ):
                coefs[(kind * OWN + q) * 4 + j] = value
    for i in range(STEPS):
        sea[place(i)] = received(i, OWN)
        for q in range(OWN):
            state[place(i), q] = received(i, q)

    def coef(kind, q, i):
        return coefs[(kind * OWN + q) * 4 + i // 8]

    def flux(kind, q, i, value, slope):
        return coef(kind, q, i) * value + coef(kind + 1, q, i) * slope

    for step in range(SUBSTEPS):
        here, prev, last, flow = [], [], [], []
        for q in range(OWN):
            start = state[0, q]
            end = state[STEPS - 1, q]
            beyond = after(start)
            slope = minmod(end - state[STEPS - 2, q], beyond - end)
            here.append(start)
            prev.append(start - before(end))
            last.append(beyond)
            flow.append(before(flux(0, q, STEPS - 1, end, slope)))
        for i in range(STEPS):
            for q in range(OWN):
                upper = state[i + 1, q] if i + 1 < STEPS else last[q]
                diff = upper - here[q]
                leaving = flux(0, q, i, here[q], minmod(prev[q], diff))
                value = here[q] - leaving + flow[q]
                here[q], prev[q], flow[q] = upper, diff, leaving
                lower = value - pltpu.roll(value, upwind, 1)
                higher = pltpu.roll(value, downwind, 1) - value
                leaving = flux(2, q, i, value, minmod(lower, higher))
                value = value - leaving + pltpu.roll(leaving, upwind, 1)
                state[i, q] = value * sea[i]

    def spread(row, times):
        pair = jnp.broadcast_to(row, (16, LON)).astype(jnp.bfloat16)
        return jnp.broadcast_to(pair[None], (times, 16, LON)).reshape(times * 16, LON)

    low_index = lax.broadcasted_iota(jnp.int32, (128, LON), 0).astype(jnp.float32).astype(jnp.bfloat16)
    high_index = lax.broadcasted_iota(jnp.int32, (256, LON), 0).astype(jnp.float32).astype(jnp.bfloat16)
    zero = jnp.zeros((), jnp.bfloat16)
    one = jnp.ones((), jnp.bfloat16)
    for j in range(4):
        for half in range(2):
            source = target = jnp.zeros((8, LON), jnp.float32)
            for k in range(4):
                lists = received(8 * j + 4 * half + k, OWN + 1)
                inside = (lane >= 32 * k) & (lane < 32 * k + 32)
                source = jnp.where(inside, pltpu.roll(lists, 32 * k, 1) if k else lists, source)
                target = jnp.where(inside, pltpu.roll(lists, (32 * k + 96) % LON, 1) if k != 1 else lists, target)
            source = source.astype(jnp.int32)
            target = target.astype(jnp.int32)
            source_row = source // LON
            source_col = source % LON
            target_row = target // LON
            target_step = target_row % STEPS
            low = ((target_step % 16) * 8 + target_row // STEPS).astype(jnp.float32)
            high = ((target_step // 16) * LON + target % LON).astype(jnp.float32)
            pieces = []
            for q in range(OWN):
                taken = jnp.zeros((8, LON), jnp.float32)
                for r in range(ROWS):
                    row = state[place(8 * j + r), q]
                    taken = jnp.where(source_row == r, jnp.take_along_axis(row, source_col, axis=1), taken)
                coarse = taken.astype(jnp.bfloat16).astype(jnp.float32)
                pieces += [coarse, taken - coarse]
            pieces.append(jnp.ones((8, LON), jnp.float32))
            for g in range(8):
                at = ((j * 2 + half) * 8 + g) * LON
                hit = low_index == spread(low[g : g + 1, :], 8)
                for n, piece in enumerate(pieces):
                    weighted[n * 128 : n * 128 + 128, at : at + LON] = jnp.where(hit, spread(piece[g : g + 1, :], 8), zero)
                hit = high_index == spread(high[g : g + 1, :], 16)
                columns[:, at : at + LON] = jnp.where(hit, one, zero)
    summed[...] = lax.dot_general(
        weighted[...], columns[...], (((1,), (1,)), ((), ())), preferred_element_type=jnp.float32
    )
    for i in range(STEPS):
        top = (i % 16) * 8
        left = (i // 16) * LON

        def block(n):
            return summed[n * 128 + top : n * 128 + top + 8, left : left + LON]

        share = 1.0 / (1.0 + block(2 * OWN))
        for q in range(OWN):
            merged = (state[place(i), q] + (block(2 * q) + block(2 * q + 1))) * share
            out[pl.ds(OWN * i + q, 8, stride=OWN * STEPS), :] = merged


def transport(device, owners, field):
    vmem = pl.BlockSpec(memory_space=pltpu.VMEM)
    smem = pl.BlockSpec(memory_space=pltpu.SMEM)
    return pl.pallas_call(
        transport_kernel,
        out_shape=jax.ShapeDtypeStruct((BINS, LON), jnp.float32),
        in_specs=[smem, smem, vmem],
        out_specs=vmem,
        scratch_shapes=[
            pltpu.VMEM((STEPS, OWN, 8, LON), jnp.float32),
            pltpu.VMEM((STEPS, 8, LON), jnp.float32),
            pltpu.VMEM((4 * OWN * 4, 8, LON), jnp.float32),
            pltpu.VMEM((PIECES * 128, ENTRIES), jnp.bfloat16),
            pltpu.VMEM((256, ENTRIES), jnp.bfloat16),
            pltpu.VMEM((PIECES * 128, 256), jnp.float32),
        ],
        compiler_params=pltpu.CompilerParams(vmem_limit_bytes=32 * 2**20),
    )(device, owners, field)


def shards(
    spectra,
    quad_first,
    quad_second,
    quad_output,
    owner_map,
    land_mask,
    nest_dest,
    nest_src,
    nest_into,
):
    everyone = ("space", "spec")
    spec_rank = lax.axis_index("spec")
    device = lax.axis_index("space") * lax.axis_size("spec") + spec_rank
    rank = spec_rank.reshape(1)
    sent = source_and_pack(
        rank,
        spectra.reshape(BINS, LON),
        land_mask,
        nest_dest.reshape(2, LON),
        nest_src.reshape(2, LON),
        nest_into.reshape(2, LON),
        quad_first,
        quad_second,
        quad_output,
    )
    banded = lax.all_to_all(
        sent.reshape(LAT, 1, SENT * LON), everyone, split_axis=0, concat_axis=0, tiled=True
    ).reshape(LAT * SENT, LON)
    merged = transport(device.reshape(1), owner_map, banded)
    rows = lax.all_to_all(
        merged.reshape(LAT, 1, OWN * LON), everyone, split_axis=0, concat_axis=0, tiled=True
    ).reshape(BINS, LON)
    finished = source_update(rank, rows, land_mask, quad_first, quad_second, quad_output)
    return finished.reshape(BINS, 1, LON)


def solution(mesh):
    return jax.shard_map(
        shards,
        mesh=mesh,
        in_specs=(
            P(None, ("space", "spec"), None),
            P(),
            P(),
            P(),
            P(),
            P("space", None),
            P("space"),
            P("space"),
            P("space"),
        ),
        out_specs=P(None, ("space", "spec"), None),
        check_vma=False,
    )
```

time: 113 us -> 76.8 us (0.68)
  Pallas kernels: 34.8 us -> 13.8 us
  starting transfers between devices: 26.3 us -> 16.5 us
  local copies, waits for them, and re-layouts: 9.02 us -> 0.03 us
  waiting for transfers between devices: 14.9 us -> 21.7 us
  other arithmetic: 3.54 us -> 0 us
    pallas_call x1, Pallas kernels: 29.2 us -> 8.54 us  [transport(): pl.pallas_call(transport_kernel, out_shape=jax.ShapeDtypeStruct((BINS, LO...]
    all_to_all x2 -> x1, starting transfers between devices: 26.3 us -> 16.5 us  [shards(): lax.all_to_all(sent.reshape(LAT, 1, SENT * LON), everyone, split_axis=0,...]
    unnamed x22 -> x10, local copies, waits for them, and re-layouts: 7.08 us -> 0.03 us
    all_to_all x2 -> x1, waiting for transfers between devices: 14.9 us -> 21.7 us  [shards(): lax.all_to_all(sent.reshape(LAT, 1, SENT * LON), everyone, split_axis=0,...]
    broadcast_in_dim x3 -> x0, local copies, waits for them, and re-layouts: 1.71 us -> none  [the longest x2 0.93 us: shards(): jnp.broadcast_to(coefs[..., None], coefs.shape + (LON,)).reshape(-1, LON)]
    all_to_all x1, blocking collectives: 23.2 us -> 24.3 us  [shards(): lax.all_to_all(merged.reshape(LAT, 1, OWN * LON), everyone, split_axis=0,...]
  transfers between devices with their start and end apart: 2 -> 1, of which waited for: 1 -> 1; matrix products, arithmetic and copies ran while one was open for 3% -> 0% of each run, Pallas kernels for 2% -> 0%
where the time goes in v2:
time: 76.8 us; the launch traced here: 76.6 us
  blocking collectives  24.3 us (32%)
  waiting for transfers between devices  21.7 us (28%)
  starting transfers between devices  16.5 us (21%)
  Pallas kernels  13.8 us (18%)
    all_to_all x1, blocking collectives, shards(): lax.all_to_all(merged.reshape(LAT, 1, OWN * LON), everyone, split_axis=0,...  24.3 us
    all_to_all x1, waiting for transfers between devices, shards(): lax.all_to_all(sent.reshape(LAT, 1, SENT * LON), everyone, split_axis=0,...  21.7 us
    all_to_all x1, starting transfers between devices, shards(): lax.all_to_all(sent.reshape(LAT, 1, SENT * LON), everyone, split_axis=0,...  16.5 us
    pallas_call x1, Pallas kernels, transport(): pl.pallas_call(transport_kernel, out_shape=jax.ShapeDtypeStruct((BINS, LO...  8.54 us
    pallas_call x1, Pallas kernels, source_and_pack(): pl.pallas_call(send_kernel, out_shape=jax.ShapeDtypeStruct((LAT * SENT, L...  3.68 us
    pallas_call x1, Pallas kernels, source_update(): pl.pallas_call(finish_kernel, out_shape=jax.ShapeDtypeStruct((BINS, LON),...  1.62 us
  transfers between devices with their start and end apart: 1, of which 1 were waited for; matrix products, arithmetic and copies ran while one was open for 0% of the time, Pallas kernels for 0%

profile of v2, /device:TPU:1, one launch (start us, length us, event | category | flops | bytes accessed | tf_op | source)
XLA Modules:
  0.0 76.6 jit_solution(1249712405369804464)
XLA Ops:
  0.0 0.0 copy-start.2
  0.0 3.7 %shard_map.91 = f32[1280,128]{1,0:T(8,128)} custom-call(s32[1]{0:T(128)} %bitcast.rank, f32[768,128]{1,0:T(8,128)} %bitcast.16, s32[8,128]{1,0:T(8,128)} %mask.1, s32[2,128]{1,0:T(2,128)} %bitcast.17, s32[2,128]{1,0:T(2,128)} %bitcast.18, s32[2,128]{1,0:T(2,128)} %bitcast.19, bf16[768,768]{1,0:T(8,128)(2,1)} %first.1, bf16[768,768]{1,0:T(8,128)(2,1)} %second.1, ...), custom_call_target="tpu_custom_call" | custom-call | tf_op jit(solution)/shard_map/pallas_call | solution.py:102
  3.7 0.0 copy-start.4
  3.7 0.0 copy-start.1
  3.7 16.5 %all-to-all-start = ((f32[256,1,640]{2,1,0:T(1,128)}), f32[256,1,640]{2,1,0:T(1,128)}, u32[]{:S(2)}, u32[]{:S(2)}) async-start(f32[256,1,640]{2,1,0:T(1,128)} %bitcast.15), calls=%async_computation | async-start | bytes 1310720 | tf_op jit(solution)/shard_map/all_to_all | solution.py:326
  20.3 0.0 copy-start
  20.3 0.0 copy-start.3
  20.3 21.7 %all-to-all-done = f32[256,1,640]{2,1,0:T(1,128)} async-done(((f32[256,1,640]{2,1,0:T(1,128)}), f32[256,1,640]{2,1,0:T(1,128)}, u32[]{:S(2)}, u32[]{:S(2)}) %all-to-all-start) | async-done | bytes 655392 | tf_op jit(solution)/shard_map/all_to_all | solution.py:326
  42.0 0.0 copy-done.4
  42.0 8.5 %shard_map.92 = f32[768,128]{1,0:T(8,128)S(1)} custom-call(s32[1]{0:T(128)} %bitcast.1.device, s32[32]{0:T(128)S(1)} %copy-done.4, f32[1280,128]{1,0:T(8,128)} %bitcast.7.field), custom_call_target="tpu_custom_call" | custom-call | tf_op jit(solution)/shard_map/pallas_call | solution.py:283
  50.6 24.3 %all_to_all.10 = f32[256,1,384]{2,1,0:T(1,128)S(1)} all-to-all(f32[256,1,384]{2,1,0:T(1,128)S(1)} %bitcast.13), channel_id=1, replica_groups=mesh['spec'=8,'space'=32] {'space','spec'}, dimensions={0} | all-to-all | bytes 786432 | tf_op jit(solution)/shard_map/all_to_all | solution.py:330
  74.9 0.0 copy-done.2
  74.9 0.0 copy-done.1
  74.9 0.0 copy-done
  74.9 0.0 copy-done.3
  74.9 1.6 %shard_map.93 = f32[768,128]{1,0:T(8,128)} custom-call(s32[1]{0:T(128)} %bitcast.rank, f32[768,128]{1,0:T(8,128)S(1)} %bitcast.14, s32[8,128]{1,0:T(8,128)S(1)} %copy-done.3, bf16[768,768]{1,0:T(8,128)(2,1)S(1)} %copy-done, bf16[768,768]{1,0:T(8,128)(2,1)S(1)} %copy-done.1, bf16[768,768]{1,0:T(8,128)(2,1)S(1)} %copy-done.2), custom_call_target="tpu_custom_call" | custom-call | tf_op jit(solution)/shard_map/pallas_call | solution.py:131
Async XLA Ops:
  0.0 74.9 %copy-start.2 = (bf16[768,768]{1,0:T(8,128)(2,1)S(1)}, bf16[768,768]{1,0:T(8,128)(2,1)}, u32[]{:S(2)}) copy-start(bf16[768,768]{1,0:T(8,128)(2,1)} %output.1) | copy-start | bytes 3538948
  3.7 38.3 %copy-start.4 = (s32[32]{0:T(128)S(1)}, s32[32]{0:T(128)}, u32[]{:S(2)}) copy-start(s32[32]{0:T(128)} %owners.1) | copy-start | bytes 388
  3.7 71.2 %copy-start.1 = (bf16[768,768]{1,0:T(8,128)(2,1)S(1)}, bf16[768,768]{1,0:T(8,128)(2,1)}, u32[]{:S(2)}) copy-start(bf16[768,768]{1,0:T(8,128)(2,1)} %second.1) | copy-start | bytes 3538948
  3.7 38.3 %all-to-all-start = ((f32[256,1,640]{2,1,0:T(1,128)}), f32[256,1,640]{2,1,0:T(1,128)}, u32[]{:S(2)}, u32[]{:S(2)}) async-start(f32[256,1,640]{2,1,0:T(1,128)} %bitcast.15), calls=%async_computation | async-start | bytes 1310720 | tf_op jit(solution)/shard_map/all_to_all | solution.py:326
  20.3 54.7 %copy-start = (bf16[768,768]{1,0:T(8,128)(2,1)S(1)}, bf16[768,768]{1,0:T(8,128)(2,1)}, u32[]{:S(2)}) copy-start(bf16[768,768]{1,0:T(8,128)(2,1)} %first.1) | copy-start | bytes 3538948
  20.3 54.7 %copy-start.3 = (s32[8,128]{1,0:T(8,128)S(1)}, s32[8,128]{1,0:T(8,128)}, u32[]{:S(2)}) copy-start(s32[8,128]{1,0:T(8,128)} %mask.1) | copy-start | bytes 12292

commit v3 on v2

--- a/solution.py
+++ b/solution.py
@@ -14,7 +14,7 @@
 LON = 128
 LAT = 256
 ROWS = 8
-ENTRIES = 8192
+SLOTS = 4096
 OWN = 3
 SENT = 5
 STEPS = 32
@@ -32,6 +32,27 @@
     product = (one * two).astype(jnp.bfloat16)
     wait(2)
     return jnp.dot(product, output[...], preferred_element_type=jnp.float32).T
+
+
+def slot_row(rank, dest, src, into):
+    below = lax.broadcasted_iota(jnp.int32, (LON, LON), 0)
+    along = lax.broadcasted_iota(jnp.int32, (LON, LON), 1)
+    turned = [jnp.broadcast_to(dest[h : h + 1, :], (LON, LON)).T for h in range(2)]
+    total = jnp.zeros((1, LON), jnp.int32)
+    for h in range(2):
+        same = dest[h : h + 1, :] == turned[h]
+        earlier = jnp.sum(jnp.where(same & (below < along), 1, 0), axis=0, keepdims=True)
+        if h:
+            earlier += jnp.sum(jnp.where(dest[1:2, :] == turned[0], 1, 0), axis=0, keepdims=True)
+        to = dest[h : h + 1, :]
+        mine = (to % 4 == rank // 2) & (to // 16 == rank % 2)
+        cells = src[h : h + 1, :] * (ROWS * LON) + into[h : h + 1, :]
+        key = jnp.where(mine, cells * 64 + (to // 4 % 4) * 16 + earlier, -1)
+        key = jnp.broadcast_to(key, (LON, LON)).T
+        chosen = (key >= 0) & (key % 64 == along % 64)
+        value = jnp.where(along < 64, key // (64 * ROWS * LON), key // 64 % (ROWS * LON) + 1)
+        total += jnp.sum(jnp.where(chosen, value, 0), axis=0, keepdims=True)
+    return jnp.broadcast_to(total.astype(jnp.float32), (8, LON))
 
 
 def send_kernel(
@@ -56,39 +77,36 @@
     sourced,
     sems,
 ):
-    pairs = (
-        (first_hbm, first),
-        (second_hbm, second),
-        (output_hbm, output),
+    pairs = [
+        (a.at[pl.ds(k * 256, 256), :], b.at[pl.ds(k * 256, 256), :])
+        for a, b in ((first_hbm, first), (second_hbm, second), (output_hbm, output))
+        for k in range(3)
+    ]
+    pairs += [
         (field_hbm, field),
         (mask_hbm, mask),
         (dest_hbm, dest),
         (src_hbm, src),
         (into_hbm, into),
-    )
+    ]
     copies = [pltpu.make_async_copy(a, b, sems.at[n]) for n, (a, b) in enumerate(pairs)]
-    for n in (3, 4, 5, 6, 7, 0, 1, 2):
+    small = range(9, 14)
+    for n in (*small, *range(9)):
         copies[n].start()
-    for n in (3, 4, 5, 6, 7):
+    for n in small:
         copies[n].wait()
     state = field[...]
     sea = mask[pl.ds(rank[0], 1), :].astype(jnp.float32)
-    part = rank[0] % 4
-    wanted = lax.broadcasted_iota(jnp.int32, (2, LON), 0) == rank[0] // 4
-    lane = lax.broadcasted_iota(jnp.int32, (8, LON), 1)
-
-    def entries(value, shift):
-        row = jnp.sum(jnp.where(wanted, value, 0), axis=0, keepdims=True).astype(jnp.float32)
-        return pltpu.roll(jnp.broadcast_to(row, (8, LON)), shift, 1)
-
-    lists = jnp.where(lane < 32, entries(src[...], (LON - 32 * part) % LON), 0.0)
-    target = entries(dest[...] * (ROWS * LON) + into[...], (LON + 32 - 32 * part) % LON)
-    lists = jnp.where((lane >= 32) & (lane < 64), target, lists)
+    lists = slot_row(rank[0], dest[...], src[...], into[...])
     wide = jnp.broadcast_to(sea, (8, LON))
     for n in range(LAT // 8):
         out[pl.ds(SENT * 8 * n + OWN, 8, stride=SENT), :] = wide
         out[pl.ds(SENT * 8 * n + OWN + 1, 8, stride=SENT), :] = lists
-    tendency = tendency_of(state, first, second, output, lambda n: copies[n].wait())
+    def wait(n):
+        for k in range(3):
+            copies[3 * n + k].wait()
+
+    tendency = tendency_of(state, first, second, output, wait)
     sourced[...] = (state + step_weight * tendency) * sea
     for n in range(LAT // 8):
         for q in range(OWN):
@@ -114,7 +132,7 @@
             square,
             square,
             pltpu.VMEM((BINS, LON), jnp.float32),
-            pltpu.SemaphoreType.DMA((8,)),
+            pltpu.SemaphoreType.DMA((14,)),
         ],
         compiler_params=pltpu.CompilerParams(vmem_limit_bytes=62 * 2**20),
     )(rank, field, mask, dest, src, into, first, second, output)
@@ -225,26 +243,22 @@
         pair = jnp.broadcast_to(row, (16, LON)).astype(jnp.bfloat16)
         return jnp.broadcast_to(pair[None], (times, 16, LON)).reshape(times * 16, LON)
 
-    low_index = lax.broadcasted_iota(jnp.int32, (128, LON), 0).astype(jnp.float32).astype(jnp.bfloat16)
+    low_index = lax.broadcasted_iota(jnp.int32, (32, LON), 0).astype(jnp.float32).astype(jnp.bfloat16)
     high_index = lax.broadcasted_iota(jnp.int32, (256, LON), 0).astype(jnp.float32).astype(jnp.bfloat16)
     zero = jnp.zeros((), jnp.bfloat16)
     one = jnp.ones((), jnp.bfloat16)
-    for j in range(4):
-        for half in range(2):
-            source = target = jnp.zeros((8, LON), jnp.float32)
-            for k in range(4):
-                lists = received(8 * j + 4 * half + k, OWN + 1)
-                inside = (lane >= 32 * k) & (lane < 32 * k + 32)
-                source = jnp.where(inside, pltpu.roll(lists, 32 * k, 1) if k else lists, source)
-                target = jnp.where(inside, pltpu.roll(lists, (32 * k + 96) % LON, 1) if k != 1 else lists, target)
-            source = source.astype(jnp.int32)
-            target = target.astype(jnp.int32)
+    left_half = lane < 64
+    for group in range(4):
+        for j in range(4):
+            even = received(8 * j + 2 * group, OWN + 1)
+            odd = received(8 * j + 2 * group + 1, OWN + 1)
+            source = jnp.where(left_half, even, pltpu.roll(odd, 64, 1)).astype(jnp.int32)
+            target = jnp.where(left_half, pltpu.roll(even, 64, 1), odd).astype(jnp.int32) - 1
             source_row = source // LON
             source_col = source % LON
             target_row = target // LON
-            target_step = target_row % STEPS
-            low = ((target_step % 16) * 8 + target_row // STEPS).astype(jnp.float32)
-            high = ((target_step // 16) * LON + target % LON).astype(jnp.float32)
+            low = jnp.where(target >= 0, (target_row % 4) * 8 + lane // 16, -1).astype(jnp.float32)
+            high = ((target_row // 4) * LON + target % LON).astype(jnp.float32)
             pieces = []
             for q in range(OWN):
                 taken = jnp.zeros((8, LON), jnp.float32)
@@ -253,28 +267,31 @@
                     taken = jnp.where(source_row == r, jnp.take_along_axis(row, source_col, axis=1), taken)
                 coarse = taken.astype(jnp.bfloat16).astype(jnp.float32)
                 pieces += [coarse, taken - coarse]
-            pieces.append(jnp.ones((8, LON), jnp.float32))
             for g in range(8):
-                at = ((j * 2 + half) * 8 + g) * LON
-                hit = low_index == spread(low[g : g + 1, :], 8)
+                at = (j * 8 + g) * LON
+                hit = low_index == spread(low[g : g + 1, :], 2)
                 for n, piece in enumerate(pieces):
-                    weighted[n * 128 : n * 128 + 128, at : at + LON] = jnp.where(hit, spread(piece[g : g + 1, :], 8), zero)
+                    weighted[group, n * 32 : n * 32 + 32, at : at + LON] = jnp.where(
+                        hit, spread(piece[g : g + 1, :], 2), zero
+                    )
+                weighted[group, 2 * OWN * 32 : PIECES * 32, at : at + LON] = jnp.where(hit, one, zero)
                 hit = high_index == spread(high[g : g + 1, :], 16)
-                columns[:, at : at + LON] = jnp.where(hit, one, zero)
-    summed[...] = lax.dot_general(
-        weighted[...], columns[...], (((1,), (1,)), ((), ())), preferred_element_type=jnp.float32
-    )
-    for i in range(STEPS):
-        top = (i % 16) * 8
-        left = (i // 16) * LON
-
-        def block(n):
-            return summed[n * 128 + top : n * 128 + top + 8, left : left + LON]
-
-        share = 1.0 / (1.0 + block(2 * OWN))
-        for q in range(OWN):
-            merged = (state[place(i), q] + (block(2 * q) + block(2 * q + 1))) * share
-            out[pl.ds(OWN * i + q, 8, stride=OWN * STEPS), :] = merged
+                columns[group, :, at : at + LON] = jnp.where(hit, one, zero)
+        summed[group] = lax.dot_general(
+            weighted[group], columns[group], (((1,), (1,)), ((), ())), preferred_element_type=jnp.float32
+        )
+        for r in range(ROWS):
+            i = 8 * group + r
+            top = (r % 4) * 8
+            left = (r // 4) * LON
+
+            def block(n):
+                return summed[group, n * 32 + top : n * 32 + top + 8, left : left + LON]
+
+            share = 1.0 / (1.0 + block(2 * OWN))
+            for q in range(OWN):
+                merged = (state[place(i), q] + (block(2 * q) + block(2 * q + 1))) * share
+                out[pl.ds(OWN * i + q, 8, stride=OWN * STEPS), :] = merged
 
 
 def transport(device, owners, field):
@@ -289,9 +306,9 @@
             pltpu.VMEM((STEPS, OWN, 8, LON), jnp.float32),
             pltpu.VMEM((STEPS, 8, LON), jnp.float32),
             pltpu.VMEM((4 * OWN * 4, 8, LON), jnp.float32),
-            pltpu.VMEM((PIECES * 128, ENTRIES), jnp.bfloat16),
-            pltpu.VMEM((256, ENTRIES), jnp.bfloat16),
-            pltpu.VMEM((PIECES * 128, 256), jnp.float32),
+            pltpu.VMEM((4, PIECES * 32, SLOTS), jnp.bfloat16),
+            pltpu.VMEM((4, 256, SLOTS), jnp.bfloat16),
+            pltpu.VMEM((4, PIECES * 32, 256), jnp.float32),
         ],
         compiler_params=pltpu.CompilerParams(vmem_limit_bytes=32 * 2**20),
     )(device, owners, field)

time: 76.8 us -> 76.9 us (level)
  no operation moved by 1% of the time
where the time goes in v3:
time: 76.9 us; the launch traced here: 76.8 us
  blocking collectives  24.3 us (32%)
  waiting for transfers between devices  21.7 us (28%)
  starting transfers between devices  16.5 us (21%)
  Pallas kernels  14 us (18%)
    all_to_all x1, blocking collectives, shards(): lax.all_to_all(merged.reshape(LAT, 1, OWN * LON), everyone, split_axis=0,...  24.3 us
    all_to_all x1, waiting for transfers between devices, shards(): lax.all_to_all(sent.reshape(LAT, 1, SENT * LON), everyone, split_axis=0,...  21.7 us
    all_to_all x1, starting transfers between devices, shards(): lax.all_to_all(sent.reshape(LAT, 1, SENT * LON), everyone, split_axis=0,...  16.5 us
    pallas_call x1, Pallas kernels, transport(): pl.pallas_call(transport_kernel, out_shape=jax.ShapeDtypeStruct((BINS, LO...  8.7 us
    pallas_call x1, Pallas kernels, source_and_pack(): pl.pallas_call(send_kernel, out_shape=jax.ShapeDtypeStruct((LAT * SENT, L...  3.7 us
    pallas_call x1, Pallas kernels, source_update(): pl.pallas_call(finish_kernel, out_shape=jax.ShapeDtypeStruct((BINS, LON),...  1.63 us
  transfers between devices with their start and end apart: 1, of which 1 were waited for; matrix products, arithmetic and copies ran while one was open for 0% of the time, Pallas kernels for 0%

profile of v3, /device:TPU:1, one launch (start us, length us, event | category | flops | bytes accessed | tf_op | source)
XLA Modules:
  0.0 76.8 jit_solution(6152490996819753797)
XLA Ops:
  0.0 0.0 copy-start.2
  0.0 3.7 %shard_map.91 = f32[1280,128]{1,0:T(8,128)} custom-call(s32[1]{0:T(128)} %bitcast.rank, f32[768,128]{1,0:T(8,128)} %bitcast.16, s32[8,128]{1,0:T(8,128)} %mask.1, s32[2,128]{1,0:T(2,128)} %bitcast.17, s32[2,128]{1,0:T(2,128)} %bitcast.18, s32[2,128]{1,0:T(2,128)} %bitcast.19, bf16[768,768]{1,0:T(8,128)(2,1)} %first.1, bf16[768,768]{1,0:T(8,128)(2,1)} %second.1, ...), custom_call_target="tpu_custom_call" | custom-call | tf_op jit(solution)/shard_map/pallas_call | solution.py:120
  3.7 0.0 copy-start.4
  3.7 0.0 copy-start.1
  3.7 16.5 %all-to-all-start = ((f32[256,1,640]{2,1,0:T(1,128)}), f32[256,1,640]{2,1,0:T(1,128)}, u32[]{:S(2)}, u32[]{:S(2)}) async-start(f32[256,1,640]{2,1,0:T(1,128)} %bitcast.15), calls=%async_computation | async-start | bytes 1310720 | tf_op jit(solution)/shard_map/all_to_all | solution.py:343
  20.3 0.0 copy-start
  20.3 0.0 copy-start.3
  20.3 21.7 %all-to-all-done = f32[256,1,640]{2,1,0:T(1,128)} async-done(((f32[256,1,640]{2,1,0:T(1,128)}), f32[256,1,640]{2,1,0:T(1,128)}, u32[]{:S(2)}, u32[]{:S(2)}) %all-to-all-start) | async-done | bytes 655392 | tf_op jit(solution)/shard_map/all_to_all | solution.py:343
  42.0 0.0 copy-done.4
  42.1 8.7 %shard_map.92 = f32[768,128]{1,0:T(8,128)S(1)} custom-call(s32[1]{0:T(128)} %bitcast.1.device, s32[32]{0:T(128)S(1)} %copy-done.4, f32[1280,128]{1,0:T(8,128)} %bitcast.7.field), custom_call_target="tpu_custom_call" | custom-call | tf_op jit(solution)/shard_map/pallas_call | solution.py:300
  50.8 24.3 %all_to_all.10 = f32[256,1,384]{2,1,0:T(1,128)S(1)} all-to-all(f32[256,1,384]{2,1,0:T(1,128)S(1)} %bitcast.13), channel_id=1, replica_groups=mesh['spec'=8,'space'=32] {'space','spec'}, dimensions={0} | all-to-all | bytes 786432 | tf_op jit(solution)/shard_map/all_to_all | solution.py:347
  75.1 0.0 copy-done.2
  75.1 0.0 copy-done.1
  75.1 0.0 copy-done
  75.1 0.0 copy-done.3
  75.1 1.6 %shard_map.93 = f32[768,128]{1,0:T(8,128)} custom-call(s32[1]{0:T(128)} %bitcast.rank, f32[768,128]{1,0:T(8,128)S(1)} %bitcast.14, s32[8,128]{1,0:T(8,128)S(1)} %copy-done.3, bf16[768,768]{1,0:T(8,128)(2,1)S(1)} %copy-done, bf16[768,768]{1,0:T(8,128)(2,1)S(1)} %copy-done.1, bf16[768,768]{1,0:T(8,128)(2,1)S(1)} %copy-done.2), custom_call_target="tpu_custom_call" | custom-call | tf_op jit(solution)/shard_map/pallas_call | solution.py:149
Async XLA Ops:
  0.0 75.1 %copy-start.2 = (bf16[768,768]{1,0:T(8,128)(2,1)S(1)}, bf16[768,768]{1,0:T(8,128)(2,1)}, u32[]{:S(2)}) copy-start(bf16[768,768]{1,0:T(8,128)(2,1)} %output.1) | copy-start | bytes 3538948
  3.7 38.3 %copy-start.4 = (s32[32]{0:T(128)S(1)}, s32[32]{0:T(128)}, u32[]{:S(2)}) copy-start(s32[32]{0:T(128)} %owners.1) | copy-start | bytes 388
  3.7 71.4 %copy-start.1 = (bf16[768,768]{1,0:T(8,128)(2,1)S(1)}, bf16[768,768]{1,0:T(8,128)(2,1)}, u32[]{:S(2)}) copy-start(bf16[768,768]{1,0:T(8,128)(2,1)} %second.1) | copy-start | bytes 3538948
  3.7 38.3 %all-to-all-start = ((f32[256,1,640]{2,1,0:T(1,128)}), f32[256,1,640]{2,1,0:T(1,128)}, u32[]{:S(2)}, u32[]{:S(2)}) async-start(f32[256,1,640]{2,1,0:T(1,128)} %bitcast.15), calls=%async_computation | async-start | bytes 1310720 | tf_op jit(solution)/shard_map/all_to_all | solution.py:343
  20.3 54.8 %copy-start = (bf16[768,768]{1,0:T(8,128)(2,1)S(1)}, bf16[768,768]{1,0:T(8,128)(2,1)}, u32[]{:S(2)}) copy-start(bf16[768,768]{1,0:T(8,128)(2,1)} %first.1) | copy-start | bytes 3538948
  20.3 54.8 %copy-start.3 = (s32[8,128]{1,0:T(8,128)S(1)}, s32[8,128]{1,0:T(8,128)}, u32[]{:S(2)}) copy-start(s32[8,128]{1,0:T(8,128)} %mask.1) | copy-start | bytes 12292

commit v4 on v3

--- a/solution.py
+++ b/solution.py
@@ -14,7 +14,6 @@
 LON = 128
 LAT = 256
 ROWS = 8
-SLOTS = 4096
 OWN = 3
 SENT = 5
 STEPS = 32
@@ -56,7 +55,7 @@
 
 
 def send_kernel(
-    rank,
+    device,
     field_hbm,
     mask_hbm,
     dest_hbm,
@@ -96,8 +95,9 @@
     for n in small:
         copies[n].wait()
     state = field[...]
-    sea = mask[pl.ds(rank[0], 1), :].astype(jnp.float32)
-    lists = slot_row(rank[0], dest[...], src[...], into[...])
+    rank = device[0] % ROWS
+    sea = mask[pl.ds(rank, 1), :].astype(jnp.float32)
+    lists = slot_row(rank, dest[...], src[...], into[...])
     wide = jnp.broadcast_to(sea, (8, LON))
     for n in range(LAT // 8):
         out[pl.ds(SENT * 8 * n + OWN, 8, stride=SENT), :] = wide
@@ -138,9 +138,10 @@
     )(rank, field, mask, dest, src, into, first, second, output)
 
 
-def finish_kernel(rank, field, mask, first, second, output, out):
+def finish_kernel(device, field, mask, first, second, output, out):
     state = field[...]
-    sea = mask[pl.ds(rank[0], 1), :].astype(jnp.float32)
+    rank = device[0] % ROWS
+    sea = mask[pl.ds(rank, 1), :].astype(jnp.float32)
     out[...] = (state + step_weight * tendency_of(state, first, second, output, lambda n: None)) * sea
 
 
@@ -159,7 +160,7 @@
     return jnp.maximum(jnp.minimum(upper, jnp.maximum(lower, 0.0)), jnp.minimum(lower, 0.0))
 
 
-def transport_kernel(device, owners, field, out, state, sea, coefs, weighted, columns, summed):
+def transport_kernel(device, owners, field, out, state, sea, coefs, summed):
     first_bin = device[0] * OWN
     first_dir = first_bin % DIRS
     north_forward = (first_dir < DIRS // 4) | (first_dir >= DIRS - DIRS // 4)
@@ -267,19 +268,21 @@
                     taken = jnp.where(source_row == r, jnp.take_along_axis(row, source_col, axis=1), taken)
                 coarse = taken.astype(jnp.bfloat16).astype(jnp.float32)
                 pieces += [coarse, taken - coarse]
+            left_sides, right_sides = [], []
             for g in range(8):
-                at = (j * 8 + g) * LON
                 hit = low_index == spread(low[g : g + 1, :], 2)
-                for n, piece in enumerate(pieces):
-                    weighted[group, n * 32 : n * 32 + 32, at : at + LON] = jnp.where(
-                        hit, spread(piece[g : g + 1, :], 2), zero
-                    )
-                weighted[group, 2 * OWN * 32 : PIECES * 32, at : at + LON] = jnp.where(hit, one, zero)
-                hit = high_index == spread(high[g : g + 1, :], 16)
-                columns[group, :, at : at + LON] = jnp.where(hit, one, zero)
-        summed[group] = lax.dot_general(
-            weighted[group], columns[group], (((1,), (1,)), ((), ())), preferred_element_type=jnp.float32
-        )
+                parts = [jnp.where(hit, spread(piece[g : g + 1, :], 2), zero) for piece in pieces]
+                parts.append(jnp.where(hit, one, zero))
+                left_sides.append(jnp.concatenate(parts, axis=0))
+                right_sides.append(jnp.where(high_index == spread(high[g : g + 1, :], 16), one, zero))
+            part = lax.dot_general(
+                jnp.concatenate(left_sides, axis=1),
+                jnp.concatenate(right_sides, axis=1),
+                (((1,), (1,)), ((), ())),
+                preferred_element_type=jnp.float32,
+            )
+            total = part if j == 0 else total + part
+        summed[group] = total
         for r in range(ROWS):
             i = 8 * group + r
             top = (r % 4) * 8
@@ -306,8 +309,6 @@
             pltpu.VMEM((STEPS, OWN, 8, LON), jnp.float32),
             pltpu.VMEM((STEPS, 8, LON), jnp.float32),
             pltpu.VMEM((4 * OWN * 4, 8, LON), jnp.float32),
-            pltpu.VMEM((4, PIECES * 32, SLOTS), jnp.bfloat16),
-            pltpu.VMEM((4, 256, SLOTS), jnp.bfloat16),
             pltpu.VMEM((4, PIECES * 32, 256), jnp.float32),
         ],
         compiler_params=pltpu.CompilerParams(vmem_limit_bytes=32 * 2**20),
@@ -327,10 +328,9 @@
 ):
     everyone = ("space", "spec")
     spec_rank = lax.axis_index("spec")
-    device = lax.axis_index("space") * lax.axis_size("spec") + spec_rank
-    rank = spec_rank.reshape(1)
+    device = (lax.axis_index("space") * lax.axis_size("spec") + spec_rank).reshape(1)
     sent = source_and_pack(
-        rank,
+        device,
         spectra.reshape(BINS, LON),
         land_mask,
         nest_dest.reshape(2, LON),
@@ -343,11 +343,11 @@
     banded = lax.all_to_all(
         sent.reshape(LAT, 1, SENT * LON), everyone, split_axis=0, concat_axis=0, tiled=True
     ).reshape(LAT * SENT, LON)
-    merged = transport(device.reshape(1), owner_map, banded)
+    merged = transport(device, owner_map, banded)
     rows = lax.all_to_all(
         merged.reshape(LAT, 1, OWN * LON), everyone, split_axis=0, concat_axis=0, tiled=True
     ).reshape(BINS, LON)
-    finished = source_update(rank, rows, land_mask, quad_first, quad_second, quad_output)
+    finished = source_update(device, rows, land_mask, quad_first, quad_second, quad_output)
     return finished.reshape(BINS, 1, LON)
 
 

time: 76.9 us -> 73.9 us (0.961)
  blocking collectives: 24.3 us -> 62.6 us
  waiting for transfers between devices: 21.7 us -> 0 us
  starting transfers between devices: 16.5 us -> 0 us
  Pallas kernels: 14 us -> 11.1 us
    all_to_all x0 -> x1, blocking collectives: none -> 38.2 us  [shards(): lax.all_to_all(sent.reshape(LAT, 1, SENT * LON), everyone, split_axis=0,...]
    all_to_all x1 -> x0, waiting for transfers between devices: 21.7 us -> none  [shards(): lax.all_to_all(sent.reshape(LAT, 1, SENT * LON), everyone, split_axis=0,...]
    all_to_all x1 -> x0, starting transfers between devices: 16.5 us -> none  [shards(): lax.all_to_all(sent.reshape(LAT, 1, SENT * LON), everyone, split_axis=0,...]
    pallas_call x1, Pallas kernels: 8.7 us -> 5.8 us  [transport(): pl.pallas_call(transport_kernel, out_shape=jax.ShapeDtypeStruct((BINS, LO...]
  transfers between devices with their start and end apart: 1 -> 0, of which waited for: 1 -> 0; matrix products, arithmetic and copies ran while one was open for 0% -> 0% of each run, Pallas kernels for 0% -> 0%
where the time goes in v4:
time: 73.9 us; the launch traced here: 73.8 us
  blocking collectives  62.6 us (85%)
  Pallas kernels  11.1 us (15%)
    all_to_all x1, blocking collectives, shards(): lax.all_to_all(sent.reshape(LAT, 1, SENT * LON), everyone, split_axis=0,...  38.2 us
    all_to_all x1, blocking collectives, shards(): lax.all_to_all(merged.reshape(LAT, 1, OWN * LON), everyone, split_axis=0,...  24.3 us
    pallas_call x1, Pallas kernels, transport(): pl.pallas_call(transport_kernel, out_shape=jax.ShapeDtypeStruct((BINS, LO...  5.8 us
    pallas_call x1, Pallas kernels, source_and_pack(): pl.pallas_call(send_kernel, out_shape=jax.ShapeDtypeStruct((LAT * SENT, L...  3.7 us
    pallas_call x1, Pallas kernels, source_update(): pl.pallas_call(finish_kernel, out_shape=jax.ShapeDtypeStruct((BINS, LON),...  1.62 us

profile of v4, /device:TPU:1, one launch (start us, length us, event | category | flops | bytes accessed | tf_op | source)
XLA Modules:
  0.0 73.8 jit_solution(10666027167203082753)
XLA Ops:
  0.0 0.0 copy-start.2
  0.0 3.7 %shard_map.91 = f32[1280,128]{1,0:T(8,128)} custom-call(s32[1]{0:T(128)} %bitcast.device, f32[768,128]{1,0:T(8,128)} %bitcast.16, s32[8,128]{1,0:T(8,128)} %mask.1, s32[2,128]{1,0:T(2,128)} %bitcast.17, s32[2,128]{1,0:T(2,128)} %bitcast.18, s32[2,128]{1,0:T(2,128)} %bitcast.19, bf16[768,768]{1,0:T(8,128)(2,1)} %first.1, bf16[768,768]{1,0:T(8,128)(2,1)} %second.1, ...), custom_call_target="tpu_custom_call" | custom-call | tf_op jit(solution)/shard_map/pallas_call | solution.py:120
  3.7 0.0 copy-start.4
  3.7 0.0 copy-start.1
  3.7 38.2 %all_to_all.10 = f32[256,1,640]{2,1,0:T(1,128)S(1)} all-to-all(f32[256,1,640]{2,1,0:T(1,128)} %bitcast.15), channel_id=1, replica_groups=mesh['spec'=8,'space'=32] {'space','spec'}, dimensions={0} | all-to-all | bytes 1310720 | tf_op jit(solution)/shard_map/all_to_all | solution.py:343
  42.0 0.0 copy-start
  42.0 0.0 copy-start.3
  42.0 0.0 copy-done.4
  42.0 5.8 %shard_map.92 = f32[768,128]{1,0:T(8,128)S(1)} custom-call(s32[1]{0:T(128)} %bitcast.device, s32[32]{0:T(128)S(1)} %copy-done.4, f32[1280,128]{1,0:T(8,128)S(1)} %bitcast.12), custom_call_target="tpu_custom_call" | custom-call | tf_op jit(solution)/shard_map/pallas_call | solution.py:303
  47.8 24.3 %all_to_all.11 = f32[256,1,384]{2,1,0:T(1,128)S(1)} all-to-all(f32[256,1,384]{2,1,0:T(1,128)S(1)} %bitcast.13), channel_id=1, replica_groups=mesh['spec'=8,'space'=32] {'space','spec'}, dimensions={0} | all-to-all | bytes 786432 | tf_op jit(solution)/shard_map/all_to_all | solution.py:347
  72.1 0.0 copy-done.2
  72.1 0.0 copy-done.1
  72.1 0.0 copy-done
  72.1 0.0 copy-done.3
  72.1 1.6 %shard_map.93 = f32[768,128]{1,0:T(8,128)} custom-call(s32[1]{0:T(128)} %bitcast.device, f32[768,128]{1,0:T(8,128)S(1)} %bitcast.14, s32[8,128]{1,0:T(8,128)S(1)} %copy-done.3, bf16[768,768]{1,0:T(8,128)(2,1)S(1)} %copy-done, bf16[768,768]{1,0:T(8,128)(2,1)S(1)} %copy-done.1, bf16[768,768]{1,0:T(8,128)(2,1)S(1)} %copy-done.2), custom_call_target="tpu_custom_call" | custom-call | tf_op jit(solution)/shard_map/pallas_call | solution.py:150
Async XLA Ops:
  0.0 72.1 %copy-start.2 = (bf16[768,768]{1,0:T(8,128)(2,1)S(1)}, bf16[768,768]{1,0:T(8,128)(2,1)}, u32[]{:S(2)}) copy-start(bf16[768,768]{1,0:T(8,128)(2,1)} %output.1) | copy-start | bytes 3538948
  3.7 38.2 %copy-start.4 = (s32[32]{0:T(128)S(1)}, s32[32]{0:T(128)}, u32[]{:S(2)}) copy-start(s32[32]{0:T(128)} %owners.1) | copy-start | bytes 388
  3.7 68.4 %copy-start.1 = (bf16[768,768]{1,0:T(8,128)(2,1)S(1)}, bf16[768,768]{1,0:T(8,128)(2,1)}, u32[]{:S(2)}) copy-start(bf16[768,768]{1,0:T(8,128)(2,1)} %second.1) | copy-start | bytes 3538948
  42.0 30.2 %copy-start = (bf16[768,768]{1,0:T(8,128)(2,1)S(1)}, bf16[768,768]{1,0:T(8,128)(2,1)}, u32[]{:S(2)}) copy-start(bf16[768,768]{1,0:T(8,128)(2,1)} %first.1) | copy-start | bytes 3538948
  42.0 30.2 %copy-start.3 = (s32[8,128]{1,0:T(8,128)S(1)}, s32[8,128]{1,0:T(8,128)}, u32[]{:S(2)}) copy-start(s32[8,128]{1,0:T(8,128)} %mask.1) | copy-start | bytes 12292

commit v5 on v4

--- a/solution.py
+++ b/solution.py
@@ -13,6 +13,7 @@
 BINS = 768
 LON = 128
 LAT = 256
+HALF = BINS // 2
 ROWS = 8
 OWN = 3
 SENT = 5
@@ -22,15 +23,19 @@
 grid_factors = (1.0, 0.55, 0.3)
 
 
-def tendency_of(state, first, second, output, wait):
+def product_of(state, first, second, wait):
     rounded = state.T.astype(jnp.bfloat16)
     wait(0)
     one = jnp.dot(rounded, first[...], preferred_element_type=jnp.float32)
     wait(1)
     two = jnp.dot(rounded, second[...], preferred_element_type=jnp.float32)
-    product = (one * two).astype(jnp.bfloat16)
-    wait(2)
-    return jnp.dot(product, output[...], preferred_element_type=jnp.float32).T
+    return (one * two).astype(jnp.bfloat16)
+
+
+def half_update(half, product, field, output, sea):
+    at = pl.ds(half * HALF, HALF)
+    tendency = jnp.dot(product, output[:, at], preferred_element_type=jnp.float32).T
+    return (field[at, :] + step_weight * tendency) * sea
 
 
 def slot_row(rank, dest, src, into):
@@ -64,6 +69,7 @@
     first_hbm,
     second_hbm,
     output_hbm,
+    out_hbm,
     out,
     field,
     mask,
@@ -78,9 +84,10 @@
 ):
     pairs = [
         (a.at[pl.ds(k * 256, 256), :], b.at[pl.ds(k * 256, 256), :])
-        for a, b in ((first_hbm, first), (second_hbm, second), (output_hbm, output))
+        for a, b in ((first_hbm, first), (second_hbm, second))
         for k in range(3)
     ]
+    pairs += [(output_hbm.at[:, pl.ds(h * HALF, HALF)], output.at[:, pl.ds(h * HALF, HALF)]) for h in range(2)]
     pairs += [
         (field_hbm, field),
         (mask_hbm, mask),
@@ -89,8 +96,8 @@
         (into_hbm, into),
     ]
     copies = [pltpu.make_async_copy(a, b, sems.at[n]) for n, (a, b) in enumerate(pairs)]
-    small = range(9, 14)
-    for n in (*small, *range(9)):
+    small = range(8, 13)
+    for n in (*small, *range(8)):
         copies[n].start()
     for n in small:
         copies[n].wait()
@@ -102,15 +109,24 @@
     for n in range(LAT // 8):
         out[pl.ds(SENT * 8 * n + OWN, 8, stride=SENT), :] = wide
         out[pl.ds(SENT * 8 * n + OWN + 1, 8, stride=SENT), :] = lists
+
     def wait(n):
         for k in range(3):
             copies[3 * n + k].wait()
 
-    tendency = tendency_of(state, first, second, output, wait)
-    sourced[...] = (state + step_weight * tendency) * sea
-    for n in range(LAT // 8):
-        for q in range(OWN):
-            out[pl.ds(SENT * 8 * n + q, 8, stride=SENT), :] = sourced[pl.ds(OWN * 8 * n + q, 8, stride=OWN), :]
+    product = product_of(state, first, second, wait)
+    sends = []
+    for half in range(2):
+        copies[6 + half].wait()
+        sourced[pl.ds(half * HALF, HALF), :] = half_update(half, product, field, output, sea)
+        for n in range(half * LAT // 16, (half + 1) * LAT // 16):
+            for q in range(OWN):
+                out[pl.ds(SENT * 8 * n + q, 8, stride=SENT), :] = sourced[pl.ds(OWN * 8 * n + q, 8, stride=OWN), :]
+        rows = pl.ds(half * LAT * SENT // 2, LAT * SENT // 2)
+        sends.append(pltpu.make_async_copy(out.at[rows, :], out_hbm.at[rows, :], sems.at[13 + half]))
+        sends[half].start()
+    for send in sends:
+        send.wait()
 
 
 def source_and_pack(rank, field, mask, dest, src, into, first, second, output):
@@ -121,8 +137,9 @@
         send_kernel,
         out_shape=jax.ShapeDtypeStruct((LAT * SENT, LON), jnp.float32),
         in_specs=[pl.BlockSpec(memory_space=pltpu.SMEM)] + [hbm] * 8,
-        out_specs=pl.BlockSpec(memory_space=pltpu.VMEM),
+        out_specs=hbm,
         scratch_shapes=[
+            pltpu.VMEM((LAT * SENT, LON), jnp.float32),
             pltpu.VMEM((BINS, LON), jnp.float32),
             pltpu.VMEM((ROWS, LON), jnp.int32),
             pair,
@@ -132,35 +149,44 @@
             square,
             square,
             pltpu.VMEM((BINS, LON), jnp.float32),
-            pltpu.SemaphoreType.DMA((14,)),
+            pltpu.SemaphoreType.DMA((15,)),
         ],
-        compiler_params=pltpu.CompilerParams(vmem_limit_bytes=62 * 2**20),
+        compiler_params=pltpu.CompilerParams(vmem_limit_bytes=63 * 2**20),
     )(rank, field, mask, dest, src, into, first, second, output)
 
 
-def finish_kernel(device, field, mask, first, second, output, out):
-    state = field[...]
-    rank = device[0] % ROWS
-    sea = mask[pl.ds(rank, 1), :].astype(jnp.float32)
-    out[...] = (state + step_weight * tendency_of(state, first, second, output, lambda n: None)) * sea
-
-
-def source_update(rank, field, mask, first, second, output):
+def finish_kernel(device, field, mask, first, second, output, out_hbm, out, sems):
+    sea = mask[pl.ds(device[0] % ROWS, 1), :].astype(jnp.float32)
+    product = product_of(field[...], first, second, lambda n: None)
+    sends = []
+    for half in range(2):
+        at = pl.ds(half * HALF, HALF)
+        out[at, :] = half_update(half, product, field, output, sea)
+        sends.append(pltpu.make_async_copy(out.at[at, :], out_hbm.at[at, :], sems.at[half]))
+        sends[half].start()
+    for send in sends:
+        send.wait()
+
+
+def source_update(device, field, mask, first, second, output):
     vmem = pl.BlockSpec(memory_space=pltpu.VMEM)
     return pl.pallas_call(
         finish_kernel,
         out_shape=jax.ShapeDtypeStruct((BINS, LON), jnp.float32),
         in_specs=[pl.BlockSpec(memory_space=pltpu.SMEM)] + [vmem] * 5,
-        out_specs=vmem,
+        out_specs=pl.BlockSpec(memory_space=pltpu.HBM),
+        scratch_shapes=[pltpu.VMEM((BINS, LON), jnp.float32), pltpu.SemaphoreType.DMA((2,))],
         compiler_params=pltpu.CompilerParams(vmem_limit_bytes=16 * 2**20),
-    )(rank, field, mask, first, second, output)
+    )(device, field, mask, first, second, output)
 
 
 def minmod(lower, upper):
     return jnp.maximum(jnp.minimum(upper, jnp.maximum(lower, 0.0)), jnp.minimum(lower, 0.0))
 
 
-def transport_kernel(device, owners, field, out, state, sea, coefs, summed):
+def transport_kernel(device, owners, field, output_hbm, out, output, state, sea, coefs, summed, sem):
+    fetch = pltpu.make_async_copy(output_hbm, output, sem)
+    fetch.start()
     first_bin = device[0] * OWN
     first_dir = first_bin % DIRS
     north_forward = (first_dir < DIRS // 4) | (first_dir >= DIRS - DIRS // 4)
@@ -295,24 +321,26 @@
             for q in range(OWN):
                 merged = (state[place(i), q] + (block(2 * q) + block(2 * q + 1))) * share
                 out[pl.ds(OWN * i + q, 8, stride=OWN * STEPS), :] = merged
-
-
-def transport(device, owners, field):
+    fetch.wait()
+
+
+def transport(device, owners, field, output):
     vmem = pl.BlockSpec(memory_space=pltpu.VMEM)
     smem = pl.BlockSpec(memory_space=pltpu.SMEM)
     return pl.pallas_call(
         transport_kernel,
-        out_shape=jax.ShapeDtypeStruct((BINS, LON), jnp.float32),
-        in_specs=[smem, smem, vmem],
-        out_specs=vmem,
+        out_shape=[jax.ShapeDtypeStruct((BINS, LON), jnp.float32), jax.ShapeDtypeStruct((BINS, BINS), jnp.bfloat16)],
+        in_specs=[smem, smem, vmem, pl.BlockSpec(memory_space=pltpu.HBM)],
+        out_specs=[vmem, vmem],
         scratch_shapes=[
             pltpu.VMEM((STEPS, OWN, 8, LON), jnp.float32),
             pltpu.VMEM((STEPS, 8, LON), jnp.float32),
             pltpu.VMEM((4 * OWN * 4, 8, LON), jnp.float32),
             pltpu.VMEM((4, PIECES * 32, 256), jnp.float32),
+            pltpu.SemaphoreType.DMA,
         ],
         compiler_params=pltpu.CompilerParams(vmem_limit_bytes=32 * 2**20),
-    )(device, owners, field)
+    )(device, owners, field, output)
 
 
 def shards(
@@ -343,11 +371,11 @@
     banded = lax.all_to_all(
         sent.reshape(LAT, 1, SENT * LON), everyone, split_axis=0, concat_axis=0, tiled=True
     ).reshape(LAT * SENT, LON)
-    merged = transport(device, owner_map, banded)
+    merged, output = transport(device, owner_map, banded, quad_output)
     rows = lax.all_to_all(
         merged.reshape(LAT, 1, OWN * LON), everyone, split_axis=0, concat_axis=0, tiled=True
     ).reshape(BINS, LON)
-    finished = source_update(device, rows, land_mask, quad_first, quad_second, quad_output)
+    finished = source_update(device, rows, land_mask, quad_first, quad_second, output)
     return finished.reshape(BINS, 1, LON)
 
 

time: 73.9 us -> 74.3 us (level)
  no operation moved by 1% of the time
where the time goes in v5:
time: 74.3 us; the launch traced here: 74.1 us
  blocking collectives  62.5 us (84%)
  Pallas kernels  11.5 us (15%)
    all_to_all x1, blocking collectives, shards(): lax.all_to_all(sent.reshape(LAT, 1, SENT * LON), everyone, split_axis=0,...  38.2 us
    all_to_all x1, blocking collectives, shards(): lax.all_to_all(merged.reshape(LAT, 1, OWN * LON), everyone, split_axis=0,...  24.3 us
    pallas_call x1, Pallas kernels, transport(): pl.pallas_call(transport_kernel, out_shape=[jax.ShapeDtypeStruct((BINS, L...  6.09 us
    pallas_call x1, Pallas kernels, source_and_pack(): pl.pallas_call(send_kernel, out_shape=jax.ShapeDtypeStruct((LAT * SENT, L...  3.82 us
    pallas_call x1, Pallas kernels, source_update(): pl.pallas_call(finish_kernel, out_shape=jax.ShapeDtypeStruct((BINS, LON),...  1.61 us

profile of v5, /device:TPU:1, one launch (start us, length us, event | category | flops | bytes accessed | tf_op | source)
XLA Modules:
  0.0 74.1 jit_solution(14475988062690523673)
XLA Ops:
  0.0 3.8 %shard_map.91 = f32[1280,128]{1,0:T(8,128)} custom-call(s32[1]{0:T(128)} %bitcast.device, f32[768,128]{1,0:T(8,128)} %bitcast.16, s32[8,128]{1,0:T(8,128)} %mask.1, s32[2,128]{1,0:T(2,128)} %bitcast.17, s32[2,128]{1,0:T(2,128)} %bitcast.18, s32[2,128]{1,0:T(2,128)} %bitcast.19, bf16[768,768]{1,0:T(8,128)(2,1)} %first.1, bf16[768,768]{1,0:T(8,128)(2,1)} %second.1, ...), custom_call_target="tpu_custom_call" | custom-call | tf_op jit(solution)/shard_map/pallas_call | solution.py:136
  3.8 0.0 copy-start
  3.8 0.0 copy-start.4
  3.9 38.2 %all_to_all.10 = f32[256,1,640]{2,1,0:T(1,128)S(1)} all-to-all(f32[256,1,640]{2,1,0:T(1,128)} %bitcast.15), channel_id=1, replica_groups=mesh['spec'=8,'space'=32] {'space','spec'}, dimensions={0} | all-to-all | bytes 1310720 | tf_op jit(solution)/shard_map/all_to_all | solution.py:371
  42.1 0.0 copy-done
  42.1 0.0 copy-done.4
  42.1 0.0 copy-start.1
  42.1 0.0 copy-start.2
  42.1 0.0 copy-start.3
  42.1 6.1 %shard_map.92 = (f32[768,128]{1,0:T(8,128)S(1)}, bf16[768,768]{1,0:T(8,128)(2,1)S(1)}) custom-call(s32[1]{0:T(128)} %bitcast.device, s32[32]{0:T(128)S(1)} %copy-done.4, f32[1280,128]{1,0:T(8,128)S(1)} %bitcast.12, bf16[768,768]{1,0:T(8,128)(2,1)S(1)} %copy-done), custom_call_target="tpu_custom_call" | custom-call | tf_op jit(solution)/shard_map/pallas_call | solution.py:330
  48.2 24.3 %all_to_all.11 = f32[256,1,384]{2,1,0:T(1,128)S(1)} all-to-all(f32[256,1,384]{2,1,0:T(1,128)S(1)} %bitcast.14), channel_id=1, replica_groups=mesh['spec'=8,'space'=32] {'space','spec'}, dimensions={0} | all-to-all | bytes 786432 | tf_op jit(solution)/shard_map/all_to_all | solution.py:375
  72.5 0.0 copy-done.1
  72.5 0.0 copy-done.2
  72.5 0.0 copy-done.3
  72.5 1.6 %shard_map.93 = f32[768,128]{1,0:T(8,128)} custom-call(s32[1]{0:T(128)} %bitcast.device, f32[768,128]{1,0:T(8,128)S(1)} %bitcast.13, s32[8,128]{1,0:T(8,128)S(1)} %copy-done.3, bf16[768,768]{1,0:T(8,128)(2,1)S(1)} %copy-done.1, bf16[768,768]{1,0:T(8,128)(2,1)S(1)} %copy-done.2, bf16[768,768]{1,0:T(8,128)(2,1)S(1)} %get-tuple-element.8.output), custom_call_target="tpu_custom_call" | custom-call | tf_op jit(solution)/shard_map/pallas_call | solution.py:173
Async XLA Ops:
  3.8 38.2 %copy-start = (bf16[768,768]{1,0:T(8,128)(2,1)S(1)}, bf16[768,768]{1,0:T(8,128)(2,1)}, u32[]{:S(2)}) copy-start(bf16[768,768]{1,0:T(8,128)(2,1)} %output_hbm.3) | copy-start | bytes 3538948
  3.8 38.2 %copy-start.4 = (s32[32]{0:T(128)S(1)}, s32[32]{0:T(128)}, u32[]{:S(2)}) copy-start(s32[32]{0:T(128)} %owners.1) | copy-start | bytes 388
  42.1 30.5 %copy-start.1 = (bf16[768,768]{1,0:T(8,128)(2,1)S(1)}, bf16[768,768]{1,0:T(8,128)(2,1)}, u32[]{:S(2)}) copy-start(bf16[768,768]{1,0:T(8,128)(2,1)} %first.1) | copy-start | bytes 3538948
  42.1 30.5 %copy-start.2 = (bf16[768,768]{1,0:T(8,128)(2,1)S(1)}, bf16[768,768]{1,0:T(8,128)(2,1)}, u32[]{:S(2)}) copy-start(bf16[768,768]{1,0:T(8,128)(2,1)} %second.1) | copy-start | bytes 3538948
  42.1 30.5 %copy-start.3 = (s32[8,128]{1,0:T(8,128)S(1)}, s32[8,128]{1,0:T(8,128)}, u32[]{:S(2)}) copy-start(s32[8,128]{1,0:T(8,128)} %mask.1) | copy-start | bytes 12292

commit v6 on v4

--- a/solution.py
+++ b/solution.py
@@ -17,7 +17,7 @@
 OWN = 3
 SENT = 5
 STEPS = 32
-PIECES = 2 * OWN + 1
+PIECES = OWN + 1
 step_weight = 0.25
 grid_factors = (1.0, 0.55, 0.3)
 
@@ -266,8 +266,7 @@
                 for r in range(ROWS):
                     row = state[place(8 * j + r), q]
                     taken = jnp.where(source_row == r, jnp.take_along_axis(row, source_col, axis=1), taken)
-                coarse = taken.astype(jnp.bfloat16).astype(jnp.float32)
-                pieces += [coarse, taken - coarse]
+                pieces.append(taken)
             left_sides, right_sides = [], []
             for g in range(8):
                 hit = low_index == spread(low[g : g + 1, :], 2)
@@ -291,9 +290,9 @@
             def block(n):
                 return summed[group, n * 32 + top : n * 32 + top + 8, left : left + LON]
 
-            share = 1.0 / (1.0 + block(2 * OWN))
+            share = 1.0 / (1.0 + block(OWN))
             for q in range(OWN):
-                merged = (state[place(i), q] + (block(2 * q) + block(2 * q + 1))) * share
+                merged = (state[place(i), q] + block(q)) * share
                 out[pl.ds(OWN * i + q, 8, stride=OWN * STEPS), :] = merged
 
 

time: 73.9 us -> 74.2 us (level)
  no operation moved by 1% of the time
where the time goes in v6:
time: 74.2 us; the launch traced here: 74.1 us
  blocking collectives  62.6 us (84%)
  Pallas kernels  11.4 us (15%)
    all_to_all x1, blocking collectives, shards(): lax.all_to_all(sent.reshape(LAT, 1, SENT * LON), everyone, split_axis=0,...  38.2 us
    all_to_all x1, blocking collectives, shards(): lax.all_to_all(merged.reshape(LAT, 1, OWN * LON), everyone, split_axis=0,...  24.3 us
    pallas_call x1, Pallas kernels, transport(): pl.pallas_call(transport_kernel, out_shape=jax.ShapeDtypeStruct((BINS, LO...  6.11 us
    pallas_call x1, Pallas kernels, source_and_pack(): pl.pallas_call(send_kernel, out_shape=jax.ShapeDtypeStruct((LAT * SENT, L...  3.7 us
    pallas_call x1, Pallas kernels, source_update(): pl.pallas_call(finish_kernel, out_shape=jax.ShapeDtypeStruct((BINS, LON),...  1.63 us

profile of v6, /device:TPU:1, one launch (start us, length us, event | category | flops | bytes accessed | tf_op | source)
XLA Modules:
  0.0 74.1 jit_solution(18147707821730676534)
XLA Ops:
  0.0 0.0 copy-start.2
  0.0 3.7 %shard_map.91 = f32[1280,128]{1,0:T(8,128)} custom-call(s32[1]{0:T(128)} %bitcast.device, f32[768,128]{1,0:T(8,128)} %bitcast.16, s32[8,128]{1,0:T(8,128)} %mask.1, s32[2,128]{1,0:T(2,128)} %bitcast.17, s32[2,128]{1,0:T(2,128)} %bitcast.18, s32[2,128]{1,0:T(2,128)} %bitcast.19, bf16[768,768]{1,0:T(8,128)(2,1)} %first.1, bf16[768,768]{1,0:T(8,128)(2,1)} %second.1, ...), custom_call_target="tpu_custom_call" | custom-call | tf_op jit(solution)/shard_map/pallas_call | solution.py:120
  3.7 0.0 copy-start.4
  3.7 0.0 copy-start.1
  3.7 38.2 %all_to_all.10 = f32[256,1,640]{2,1,0:T(1,128)S(1)} all-to-all(f32[256,1,640]{2,1,0:T(1,128)} %bitcast.15), channel_id=1, replica_groups=mesh['spec'=8,'space'=32] {'space','spec'}, dimensions={0} | all-to-all | bytes 1310720 | tf_op jit(solution)/shard_map/all_to_all | solution.py:342
  42.0 0.0 copy-start
  42.0 0.0 copy-start.3
  42.0 0.0 copy-done.4
  42.0 6.1 %shard_map.92 = f32[768,128]{1,0:T(8,128)S(1)} custom-call(s32[1]{0:T(128)} %bitcast.device, s32[32]{0:T(128)S(1)} %copy-done.4, f32[1280,128]{1,0:T(8,128)S(1)} %bitcast.12), custom_call_target="tpu_custom_call" | custom-call | tf_op jit(solution)/shard_map/pallas_call | solution.py:302
  48.1 24.3 %all_to_all.11 = f32[256,1,384]{2,1,0:T(1,128)S(1)} all-to-all(f32[256,1,384]{2,1,0:T(1,128)S(1)} %bitcast.13), channel_id=1, replica_groups=mesh['spec'=8,'space'=32] {'space','spec'}, dimensions={0} | all-to-all | bytes 786432 | tf_op jit(solution)/shard_map/all_to_all | solution.py:346
  72.4 0.0 copy-done.2
  72.4 0.0 copy-done.1
  72.4 0.0 copy-done
  72.4 0.0 copy-done.3
  72.4 1.6 %shard_map.93 = f32[768,128]{1,0:T(8,128)} custom-call(s32[1]{0:T(128)} %bitcast.device, f32[768,128]{1,0:T(8,128)S(1)} %bitcast.14, s32[8,128]{1,0:T(8,128)S(1)} %copy-done.3, bf16[768,768]{1,0:T(8,128)(2,1)S(1)} %copy-done, bf16[768,768]{1,0:T(8,128)(2,1)S(1)} %copy-done.1, bf16[768,768]{1,0:T(8,128)(2,1)S(1)} %copy-done.2), custom_call_target="tpu_custom_call" | custom-call | tf_op jit(solution)/shard_map/pallas_call | solution.py:150
Async XLA Ops:
  0.0 72.4 %copy-start.2 = (bf16[768,768]{1,0:T(8,128)(2,1)S(1)}, bf16[768,768]{1,0:T(8,128)(2,1)}, u32[]{:S(2)}) copy-start(bf16[768,768]{1,0:T(8,128)(2,1)} %output.1) | copy-start | bytes 3538948
  3.7 38.2 %copy-start.4 = (s32[32]{0:T(128)S(1)}, s32[32]{0:T(128)}, u32[]{:S(2)}) copy-start(s32[32]{0:T(128)} %owners.1) | copy-start | bytes 388
  3.7 68.7 %copy-start.1 = (bf16[768,768]{1,0:T(8,128)(2,1)S(1)}, bf16[768,768]{1,0:T(8,128)(2,1)}, u32[]{:S(2)}) copy-start(bf16[768,768]{1,0:T(8,128)(2,1)} %second.1) | copy-start | bytes 3538948
  42.0 30.5 %copy-start = (bf16[768,768]{1,0:T(8,128)(2,1)S(1)}, bf16[768,768]{1,0:T(8,128)(2,1)}, u32[]{:S(2)}) copy-start(bf16[768,768]{1,0:T(8,128)(2,1)} %first.1) | copy-start | bytes 3538948
  42.0 30.5 %copy-start.3 = (s32[8,128]{1,0:T(8,128)S(1)}, s32[8,128]{1,0:T(8,128)}, u32[]{:S(2)}) copy-start(s32[8,128]{1,0:T(8,128)} %mask.1) | copy-start | bytes 12292
